TPU v7x, 128 devices: a whole 4x4x4 slice. The times are simulated.
128 devices in a mesh: row: 4 (over y), col: 16 (over x, z_lo, core), depth: 2 (over z_hi).
Axes of the slice: x: 4, y: 4, z: 4 (z_hi: 2, z_lo: 2; z = z_hi * 2 + z_lo), core: 2. Of those that a mesh axis runs over, the one named last changes fastest.
Arguments:
- features: bfloat16 [32768, 128], P(('row', 'col')), may hold values from -6 to 6
- self_weight: bfloat16 [128, 256], P(None, 'depth'), may hold values from -0.5 to 0.5
- neigh_weight: bfloat16 [128, 256], P(None, 'depth'), may hold values from -0.5 to 0.5
- bias: float32 [256], P('depth'), may hold values from -3 to 3
- cotangent: bfloat16 [32768, 256], P(('row', 'col'), 'depth'), may hold values from -6 to 6
- tile_values: bfloat16 [32768, 128, 128], P(('row', 'col', 'depth')), may hold values from -0.0625 to 0.0625
- tile_rows: int32 [128, 256], P(('row', 'col', 'depth')), may hold values from 0 to 63
- tile_cols: int32 [128, 256], P(('row', 'col', 'depth')), may hold values from 0 to 15
- tile_counts: int32 [128], P(('row', 'col', 'depth')), may hold values from 32 to 256, as said below
Outputs:
- output: bfloat16 [32768, 256], P(('row', 'col'), 'depth')
- grad_features: bfloat16 [32768, 128], P(('row', 'col', 'depth'))
- grad_self: float32 [128, 256], P(None, 'depth')
- grad_neigh: float32 [128, 256], P(None, 'depth')
- grad_bias: float32 [256], P('depth')
Inputs may be any that keep to these rules, and one draw needn't show every extreme that they name: `tile_rows`: a row block below 64. `tile_cols`: a column block below 16. `tile_counts`: each device's count is 256 divided by 1, 2, 4 or 8; some device has all 256 slots live.
All inputs are finite; a program needn't handle non-finite values.
Results may differ from a plain program's by a relative error of at most 0.0057.
Values may be sent and summed in bfloat16 or wider, within the bound.
No kernel may reach another device: no remote copies, remote signals or barrier semaphores. Data moves between devices by JAX's collectives and lax.ppermute only.
A program may use at most 64 MiB of HBM per device.

v0:
```python
import jax
import jax.numpy as jnp
from jax import lax
from jax.sharding import PartitionSpec as P


def accumulate(
    tile_values,
    out_blocks,
    in_blocks,
    live_mask,
    source,
    block_count,
    forward,
    group_bound,
    group_size,
):
    block_size = tile_values.shape[1]
    hidden = source.shape[1]
    source_blocks = source.reshape(-1, block_size, hidden)

    def add_group(group_index, totals):
        offset = group_index * group_size
        tile_block = lax.dynamic_slice_in_dim(tile_values, offset, group_size, 0)
        out_index = lax.dynamic_slice_in_dim(out_blocks, offset, group_size, 0)
        in_index = lax.dynamic_slice_in_dim(in_blocks, offset, group_size, 0)
        alive = lax.dynamic_slice_in_dim(live_mask, offset, group_size, 0)
        if forward:
            product = jnp.einsum(
                "tij,tjh->tih",
                tile_block,
                source_blocks[in_index],
                preferred_element_type=jnp.float32,
            )
            target = out_index
        else:
            product = jnp.einsum(
                "tij,tih->tjh",
                tile_block,
                source_blocks[out_index],
                preferred_element_type=jnp.float32,
            )
            target = in_index
        product = jnp.where(alive[:, None, None], product, 0.0)
        return totals.at[target].add(product)

    totals = jnp.zeros((block_count, block_size, hidden), jnp.float32)
    totals = lax.fori_loop(0, group_bound, add_group, totals)
    return totals.reshape(block_count * block_size, hidden)


def body(
    features,
    self_weight,
    neigh_weight,
    bias,
    cotangent,
    tile_values,
    tile_rows,
    tile_cols,
    tile_counts,
):
    span_rows = features.shape[0]
    block_size = tile_values.shape[1]
    tile_slots = tile_values.shape[0]
    row_count = lax.axis_size("row")
    col_count = lax.axis_size("col")
    out_blocks = tile_rows[0]
    in_blocks = tile_cols[0]
    live_count = tile_counts[0]
    live_mask = jnp.arange(tile_slots, dtype=jnp.int32) < live_count
    group_size = 32
    group_bound = tile_slots // group_size
    transformed = jnp.dot(features, neigh_weight, preferred_element_type=jnp.float32).astype(
        jnp.bfloat16
    )
    transformed = lax.all_gather(transformed, "depth", axis=1, tiled=True)
    column_source = lax.all_gather(transformed, "row", axis=0, tiled=True)
    row_blocks = span_rows * col_count // block_size
    partial_value = accumulate(
        tile_values,
        out_blocks,
        in_blocks,
        live_mask,
        column_source,
        row_blocks,
        True,
        group_bound,
        group_size,
    )
    aggregated = lax.psum_scatter(partial_value, "col", scatter_dimension=0, tiled=True)
    aggregated = lax.psum_scatter(aggregated, "depth", scatter_dimension=1, tiled=True)
    preact = jnp.dot(features, self_weight, preferred_element_type=jnp.float32) + aggregated + bias
    gate_value = jax.nn.sigmoid(preact)
    output = (preact * gate_value).astype(jnp.bfloat16)
    grad_pre = (
        cotangent.astype(jnp.float32) * gate_value * (1.0 + preact * (1.0 - gate_value))
    ).astype(jnp.bfloat16)
    grad_rows = lax.all_gather(grad_pre, "depth", axis=1, tiled=True)
    grad_rows = lax.all_gather(grad_rows, "col", axis=0, tiled=True)
    column_blocks = span_rows * row_count // block_size
    grad_partial = accumulate(
        tile_values,
        out_blocks,
        in_blocks,
        live_mask,
        grad_rows,
        column_blocks,
        False,
        group_bound,
        group_size,
    )
    grad_partial = lax.psum_scatter(grad_partial, "depth", scatter_dimension=1, tiled=True)
    grad_transformed = lax.psum_scatter(
        grad_partial, "row", scatter_dimension=0, tiled=True
    ).astype(jnp.bfloat16)
    input_terms = jnp.dot(grad_pre, self_weight.T, preferred_element_type=jnp.float32) + jnp.dot(
        grad_transformed, neigh_weight.T, preferred_element_type=jnp.float32
    )
    grad_features = lax.psum_scatter(input_terms, "depth", scatter_dimension=0, tiled=True).astype(
        jnp.bfloat16
    )
    contract = (((0,), (0,)), ((), ()))
    self_local = lax.dot_general(features, grad_pre, contract, preferred_element_type=jnp.float32)
    neigh_local = lax.dot_general(
        features, grad_transformed, contract, preferred_element_type=jnp.float32
    )
    bias_local = jnp.sum(grad_pre.astype(jnp.float32), axis=0)
    grad_self, grad_neigh, grad_bias = lax.psum(
        (self_local, neigh_local, bias_local), ("row", "col")
    )
    grad_scale = 1.0 / jnp.sqrt(jnp.float32(span_rows * row_count * col_count))
    return (
        output,
        grad_features,
        grad_self * grad_scale,
        grad_neigh * grad_scale,
        grad_bias * grad_scale,
    )


def solution(mesh):
    placed = (
        P(("row", "col"), None),
        P(None, "depth"),
        P(None, "depth"),
        P("depth"),
        P(("row", "col"), "depth"),
        P(("row", "col", "depth"), None, None),
        P(("row", "col", "depth"), None),
        P(("row", "col", "depth"), None),
        P(("row", "col", "depth")),
    )
    return jax.shard_map(
        body,
        mesh=mesh,
        in_specs=placed,
        out_specs=(
            P(("row", "col"), "depth"),
            P(("row", "col", "depth"), None),
            P(None, "depth"),
            P(None, "depth"),
            P("depth"),
        ),
        check_vma=False,
    )
```

profile of v0, /device:TPU:4, one launch (start us, length us, event | category | flops | bytes accessed | tf_op | source)
XLA Modules:
  0.0 1033.7 jit_solution(4848484001516112475)
XLA Ops:
  9.0 8.2 all_gather.12
  17.9 25.3 %all-gather.3.cloned.1.call-done = bf16[2048,256]{1,0:T(8,128)(2,1)} async-done(((bf16[512,256]{1,0:T(8,128)(2,1)}), bf16[2048,256]{1,0:T(8,128)(2,1)}) %all-gather.3.cloned.1.call-update) | async-done | bytes 1048592 | tf_op jit(solution)/shard_map/all_gather | solution.py:78
  47.5 118.3 %while.26 = (s32[]{:T(128)}, f32[64,128,256]{2,1,0:T(8,128)}, s32[256]{0:T(256)S(1)}, pred[256]{0:T(512)(128)(4,1)S(1)}, bf16[256,128,128]{2,1,0:T(8,128)(2,1)},...) while((s32[]{:T(128)}, f32[64,128,256]{2,1,0:T(8,128)}, ...), condition=%wide.region_2.3_spmd, body=%wide.region_0.2_spmd.sunk | while | flops 270533824 | bytes 24122504 | solution.py:48
  52.2 10.1 scatter_fusion
  67.0 10.0 scatter_fusion
  81.8 10.1 scatter_fusion
  96.6 10.0 scatter_fusion
  111.3 10.0 scatter_fusion
  126.1 10.0 scatter_fusion
  140.9 10.1 scatter_fusion
  155.7 10.1 scatter_fusion
  165.9 95.5 %reduce-scatter.6.cloned.1.call-done = f32[512,256]{1,0:T(8,128)} async-done(((f32[8192,256]{1,0:T(8,128)}), f32[512,256]{1,0:T(8,128)}) %reduce-scatter.6.cloned.1.call-update) | async-done | bytes 524304 | tf_op jit(solution)/shard_map/reduce_scatter | solution.py:91
  261.4 23.6 %reduce-scatter.8.cloned.1.call-done = f32[512,128]{1,0:T(8,128)} async-done(((f32[512,256]{1,0:T(8,128)}), f32[512,128]{1,0:T(8,128)}) %reduce-scatter.8.cloned.1.call-update) | async-done | bytes 262160 | tf_op jit(solution)/shard_map/reduce_scatter | solution.py:92
  286.9 7.4 all_gather.14
  294.4 35.6 %all-gather.5.cloned.1.call-done = bf16[8192,256]{1,0:T(8,128)(2,1)} async-done(((bf16[512,256]{1,0:T(8,128)(2,1)}), bf16[8192,256]{1,0:T(8,128)(2,1)}) %all-gather.5.cloned.1.call-update) | async-done | bytes 4194320 | tf_op jit(solution)/shard_map/all_gather | solution.py:100
  330.2 125.0 %while.27 = (s32[]{:T(128)}, f32[16,128,256]{2,1,0:T(8,128)S(1)}, s32[256]{0:T(256)S(1)}, pred[256]{0:T(512)(128)(4,1)S(1)}, bf16[256,128,128]{2,1,0:T(8,128)(2,...) while((s32[]{:T(128)}, f32[16,128,256]{2,1,0:T(8,128)S(1)}, ...), condition=%wide.region_7.8_spmd, body=%wide.region_5.7_spmd.sunk | while | flops 270533824 | bytes 24122504 | solution.py:48
  339.3 6.5 scatter_fusion.1
  386.2 6.5 scatter_fusion.1
  448.7 6.5 scatter_fusion.1
  456.6 37.2 %reduce-scatter.10.cloned.1.call-done = f32[2048,128]{1,0:T(8,128)} async-done(((f32[2048,256]{1,0:T(8,128)}), f32[2048,128]{1,0:T(8,128)}) %reduce-scatter.10.cloned.1.call-update) | async-done | bytes 1048592 | tf_op jit(solution)/shard_map/reduce_scatter | solution.py:113
  495.0 24.1 %reduce-scatter.12.cloned.1.call-done = f32[512,128]{1,0:T(8,128)} async-done(((f32[2048,128]{1,0:T(8,128)}), f32[512,128]{1,0:T(8,128)}) %reduce-scatter.12.cloned.1.call-update) | async-done | bytes 262160 | tf_op jit(solution)/shard_map/reduce_scatter | solution.py:114
  522.8 118.5 %psum.23 = f32[128]{0:T(128)S(1)} all-reduce(f32[128]{0:T(128)S(1)} %get-tuple-element.297), channel_id=1, replica_groups=mesh['row'=4,'col'=16,'depth'=2] {'row','col'}, use_global_device_ids=true, to_apply=%region_14.15 | all-reduce | flops 128 | bytes 1024 | tf_op jit(solution)/shard_map/psum | solution.py:129
  641.8 356.2 %all-reduce.3.cloned.1.call-done = (f32[128,128]{0,1:T(8,128)}, f32[128,128]{0,1:T(8,128)}) async-done(((f32[128,128]{0,1:T(8,128)}, f32[128,128]{0,1:T(8,128)}), (f32[128,128]{0,1:T(8,128)}, f32[128,128]{0,1:T(8,128)})) %all-reduce.3.cloned.1.call-update) | async-done | bytes 131088 | tf_op jit(solution)/shard_map/psum | solution.py:129
  1000.4 24.9 %reduce-scatter.14.cloned.1.call-done = f32[256,128]{1,0:T(8,128)} async-done(((f32[512,128]{1,0:T(8,128)}), f32[256,128]{1,0:T(8,128)}) %reduce-scatter.14.cloned.1.call-update) | async-done | bytes 131088 | tf_op jit(solution)/shard_map/reduce_scatter | solution.py:120
  (133 shorter events, 162.1 us)
Async XLA Ops:
  7.2 0.9 copy-start
  7.2 36.0 %all-gather.3.cloned.1.call-start = ((), (), s32[]{:S(2)}) async-start(), calls=%async_computation.5 | async-start | bytes 1310720 | tf_op jit(solution)/shard_map/all_gather | solution.py:78
  17.2 244.2 %reduce-scatter.6.cloned.1.call-start = ((), (), s32[]{:S(2)}) async-start(), calls=%async_computation.6 | async-start | bytes 8912896 | tf_op jit(solution)/shard_map/reduce_scatter | solution.py:91
  43.2 4.3 copy-start.2
  43.2 4.3 copy-start.5
  43.2 4.3 copy-start.6
  165.8 119.2 %copy-start.4 = (bf16[128,128]{1,0:T(8,128)(2,1)S(1)}, bf16[128,128]{1,0:T(8,128)(2,1)}, u32[]{:S(2)}) copy-start(bf16[128,128]{1,0:T(8,128)(2,1)} %param.14) | copy-start | bytes 98308
  165.8 119.2 %copy-start.7 = (bf16[512,128]{1,0:T(8,128)(2,1)S(1)}, bf16[512,128]{1,0:T(8,128)(2,1)}, u32[]{:S(2)}) copy-start(bf16[512,128]{1,0:T(8,128)(2,1)} %param.17) | copy-start | bytes 393220
  165.8 119.2 %copy-start.8 = (f32[128]{0:T(128)S(1)}, f32[128]{0:T(128)}, u32[]{:S(2)}) copy-start(f32[128]{0:T(128)} %param.16) | copy-start | bytes 1540
  165.8 119.2 %reduce-scatter.8.cloned.1.call-start = ((), (), s32[]{:S(2)}) async-start(), calls=%async_computation.7 | async-start | bytes 786432 | tf_op jit(solution)/shard_map/reduce_scatter | solution.py:92
  261.4 68.6 %all-gather.5.cloned.1.call-start = ((), (), s32[]{:S(2)}) async-start(), calls=%async_computation.8 | async-start | bytes 4456448 | tf_op jit(solution)/shard_map/all_gather | solution.py:100
  294.3 199.5 %reduce-scatter.10.cloned.1.call-start = ((), (), s32[]{:S(2)}) async-start(), calls=%async_computation.9 | async-start | bytes 3145728 | tf_op jit(solution)/shard_map/reduce_scatter | solution.py:113
  455.2 1.3 copy-start.1
  455.2 65.7 %copy-start.3 = (bf16[128,128]{1,0:T(8,128)(2,1)S(1)}, bf16[128,128]{1,0:T(8,128)(2,1)}, u32[]{:S(2)}) copy-start(bf16[128,128]{1,0:T(8,128)(2,1)} %param.15) | copy-start | bytes 98308
  456.6 62.5 %reduce-scatter.12.cloned.1.call-start = ((), (), s32[]{:S(2)}) async-start(), calls=%async_computation.10 | async-start | bytes 1310720 | tf_op jit(solution)/shard_map/reduce_scatter | solution.py:114
  493.9 504.1 %all-reduce.3.cloned.1.call-start = ((), (), s32[]{:S(2)}) async-start(), calls=%async_computation.12 | async-start | bytes 262144 | tf_op jit(solution)/shard_map/psum | solution.py:129
  520.9 504.4 %reduce-scatter.14.cloned.1.call-start = ((), (), s32[]{:S(2)}) async-start(), calls=%async_computation.11 | async-start | bytes 393216 | tf_op jit(solution)/shard_map/reduce_scatter | solution.py:120
Sparse Core Ops, SparseCore 0:
  17.3 25.8 all-gather.2
  166.0 95.3 reduce-scatter.5
  263.7 21.2 reduce-scatter.7
  294.5 35.4 all-gather.4
  456.7 37.1 reduce-scatter.9
  496.1 22.8 reduce-scatter.11
  522.2 475.8 all-reduce.2
  1000.3 24.9 reduce-scatter.13
where the time goes:
time: 1040 us; the launch traced here: 1030 us
  waiting for transfers between devices  623 us (60%)
  other arithmetic  137 us (13%)
  blocking collectives  134 us (13%)
  matrix products  76.3 us (7%)
  local copies, waits for them, and re-layouts  48.7 us (5%)
  between operations  14.9 us (1%)
    psum x1, waiting for transfers between devices, body(): lax.psum((self_local, neigh_local, bias_local), ('row', 'col'))  356 us
    scatter-add x16, other arithmetic, add_group(): return totals.at[target].add(product)  132 us
    psum x1, blocking collectives, body(): lax.psum((self_local, neigh_local, bias_local), ('row', 'col'))  119 us
    reduce_scatter x1, waiting for transfers between devices, body(): lax.psum_scatter(partial_value, 'col', scatter_dimension=0, tiled=True)  95.5 us
    dot_general x8, matrix products, add_group(): jnp.einsum('tij,tih->tjh', tile_block, source_blocks[out_index], preferre...  37.8 us
    reduce_scatter x1, waiting for transfers between devices, body(): lax.psum_scatter(grad_partial, 'depth', scatter_dimension=1, tiled=True)  37.2 us
    all_gather x1, waiting for transfers between devices, body(): grad_rows = lax.all_gather(grad_rows, 'col', axis=0, tiled=True)  35.6 us
    gather x8, local copies, waits for them, and re-layouts, add_group(): source_blocks[out_index]  33.9 us
  transfers between devices with their start and end apart: 8, of which 8 were waited for; matrix products, arithmetic and copies ran while one was open for 1% of the time, Pallas kernels for 0%

commit v1 on v0

v1 whole, which is shorter than its diff:
```python
import jax
import jax.numpy as jnp
from jax import lax
from jax.experimental import pallas as pl
from jax.experimental.pallas import tpu as pltpu
from jax.sharding import PartitionSpec as P

GROUP = 32
UNROLL = 8
F32 = jnp.float32
BF16 = jnp.bfloat16


def dot_nn(a, b):
    return lax.dot_general(a, b, (((1,), (0,)), ((), ())), preferred_element_type=F32)


def dot_nt(a, b):
    return lax.dot_general(a, b, (((1,), (1,)), ((), ())), preferred_element_type=F32)


def dot_tn(a, b):
    return lax.dot_general(a, b, (((0,), (0,)), ((), ())), preferred_element_type=F32)


def start_tiles(live_groups, tiles, tile_buf, sems):
    def start(group, carry):
        at = pl.ds(group * GROUP, GROUP)
        pltpu.make_async_copy(tiles.at[at], tile_buf.at[at], sems.at[group]).start()
        return carry

    lax.fori_loop(0, live_groups, start, 0)


def for_tiles(live_groups, tiles, tile_buf, sems, step):
    def one_group(group, carry):
        at = pl.ds(group * GROUP, GROUP)
        pltpu.make_async_copy(tiles.at[at], tile_buf.at[at], sems.at[group]).wait()

        def some(part, inner):
            for k in range(UNROLL):
                step(group * GROUP + part * UNROLL + k)
            return inner

        return lax.fori_loop(0, GROUP // UNROLL, some, carry)

    lax.fori_loop(0, live_groups, one_group, 0)


def forward_kernel(info, rows, cols, x0, x1, x2, x3, tiles, out, x_buf, tile_buf, acc, sems, x_sems):
    live_groups = info[0] // GROUP
    own_row = info[1]
    start_tiles(live_groups, tiles, tile_buf, sems)
    shards = (x0, x1, x2, x3)
    span = x0.shape[0]
    copies = [
        pltpu.make_async_copy(shard, x_buf.at[pl.ds(k * span, span)], x_sems.at[k])
        for k, shard in enumerate(shards)
    ]
    for copy in copies:
        copy.start()
    acc[...] = jnp.zeros_like(acc)
    for copy in copies:
        copy.wait()
    span_blocks = span // 128

    def step(t):
        j = cols[t]
        at = ((own_row - j // span_blocks) & 3) * span_blocks + j % span_blocks
        block = x_buf[pl.ds(pl.multiple_of(at * 128, 128), 128), :]
        target = pl.ds(pl.multiple_of(rows[t] * 128, 128), 128)
        acc[target, :] += dot_nn(tile_buf[t], block)

    for_tiles(live_groups, tiles, tile_buf, sems, step)
    out[...] = acc[...].astype(BF16)


def backward_kernel(info, rows, cols, q, tiles, out, tile_buf, acc, sems):
    live_groups = info[0] // GROUP
    start_tiles(live_groups, tiles, tile_buf, sems)
    acc[...] = jnp.zeros_like(acc)

    def step(t):
        acc[cols[t]] += dot_nn(q[rows[t]], tile_buf[t])

    for_tiles(live_groups, tiles, tile_buf, sems, step)
    out[...] = acc[...].astype(BF16)


def middle_kernel(
    depth, parts, x, ws_a, ws_b, wn_a, wn_b, b_a, b_b, cot_a, cot_b,
    out_a, out_b, q, own_term, gw_a, gw_b,
):
    total = parts[0].astype(F32)
    for k in range(1, parts.shape[0]):
        total = total + parts[k].astype(F32)
    high = total.astype(BF16)
    low = (total - high.astype(F32)).astype(BF16)
    x_val = x[...]
    grads = []
    for ws, wn, b, cot, out in ((ws_a, wn_a, b_a, cot_a, out_a), (ws_b, wn_b, b_b, cot_b, out_b)):
        wn_val = wn[...]
        pre = dot_nn(x_val, ws[...]) + (dot_nn(high, wn_val) + dot_nn(low, wn_val)) + b[...]
        gate = jax.nn.sigmoid(pre)
        out[...] = (pre * gate).astype(BF16)
        grads.append((cot[...].astype(F32) * gate * (1.0 + pre * (1.0 - gate))).astype(BF16))
    g_a, g_b = grads
    for k in range(q.shape[0]):
        at = slice(k * 128, (k + 1) * 128)
        q[k] = (dot_nt(wn_a[...], g_a[at]) + dot_nt(wn_b[...], g_b[at])).astype(BF16)
    own_term[...] = dot_nt(g_a, ws_a[...]) + dot_nt(g_b, ws_b[...])
    for g, gw in ((g_a, gw_a), (g_b, gw_b)):
        gw[0:128] = dot_tn(x_val, g)
        gw[128:256] = dot_tn(high, g) + dot_tn(low, g)
        gw[256:264] = jnp.broadcast_to(jnp.sum(g.astype(F32), axis=0, keepdims=True), (8, 128))


def finish_kernel(parts, own_term, out):
    for k in range(parts.shape[1]):
        total = parts[0, k].astype(F32)
        for m in range(1, parts.shape[0]):
            total = total + parts[m, k].astype(F32)
        at = slice(k * 128, (k + 1) * 128)
        out[at] = (total.T + own_term[at]).astype(BF16)


def body(
    features,
    self_weight,
    neigh_weight,
    bias,
    cotangent,
    tile_values,
    tile_rows,
    tile_cols,
    tile_counts,
):
    span = features.shape[0]
    half = span // 2
    slots = tile_values.shape[0]
    row_count = lax.axis_size("row")
    col_count = lax.axis_size("col")
    depth_count = lax.axis_size("depth")
    own_row = lax.axis_index("row")
    own_depth = lax.axis_index("depth")
    swap = [(0, 1), (1, 0)]
    vmem = pl.BlockSpec(memory_space=pltpu.VMEM)
    smem = pl.BlockSpec(memory_space=pltpu.SMEM)
    hbm = pl.BlockSpec(memory_space=pl.ANY)
    scratch_tiles = pltpu.VMEM((slots, 128, 128), BF16)
    tile_sems = pltpu.SemaphoreType.DMA((slots // GROUP,))

    def from_row(k):
        return lax.ppermute(features, "row", [(i, (i + k) % row_count) for i in range(row_count)])

    shards = [features] + [from_row(k) for k in range(1, row_count)]
    other_cot = lax.ppermute(
        lax.dynamic_slice_in_dim(cotangent, (1 - own_depth) * half, half, 0), "depth", swap
    )
    other_ws = lax.ppermute(self_weight, "depth", swap)
    other_wn = lax.ppermute(neigh_weight, "depth", swap)
    own_bias = bias[None, :]
    other_bias = lax.ppermute(own_bias, "depth", swap)

    info = jnp.stack([tile_counts[0], own_row.astype(jnp.int32)])
    rows = tile_rows[0]
    cols = tile_cols[0]
    group_rows = span * col_count
    partial = pl.pallas_call(
        forward_kernel,
        in_specs=[smem] * 3 + [hbm] * 5,
        out_specs=vmem,
        out_shape=jax.ShapeDtypeStruct((group_rows, 128), BF16),
        scratch_shapes=[
            pltpu.VMEM((span * row_count, 128), BF16),
            scratch_tiles,
            pltpu.VMEM((group_rows, 128), F32),
            tile_sems,
            pltpu.SemaphoreType.DMA((row_count,)),
        ],
        name="forward",
    )(info, rows, cols, *shards, tile_values)
    plane = col_count * depth_count
    parts = lax.all_to_all(partial.reshape(plane, half, 128), ("col", "depth"), 0, 0, tiled=True)

    def mine(shape):
        return pl.BlockSpec(shape, lambda i, d: (d[0], 0))

    def whole(shape):
        return pl.BlockSpec(shape, lambda i, d: (0,) * len(shape))

    out_shapes = [
        jax.ShapeDtypeStruct((half, 128), BF16),
        jax.ShapeDtypeStruct((half, 128), BF16),
        jax.ShapeDtypeStruct((half // 128, 128, 128), BF16),
        jax.ShapeDtypeStruct((half, 128), F32),
        jax.ShapeDtypeStruct((264, 128), F32),
        jax.ShapeDtypeStruct((264, 128), F32),
    ]
    weight = whole((128, 128))
    line = whole((1, 128))
    out_own, out_other, q, own_term, gw_own, gw_other = pl.pallas_call(
        middle_kernel,
        grid_spec=pltpu.PrefetchScalarGridSpec(
            num_scalar_prefetch=1,
            grid=(1,),
            in_specs=[
                whole((plane, half, 128)),
                mine((half, 128)),
                weight, weight, weight, weight, line, line,
                mine((half, 128)),
                whole((half, 128)),
            ],
            out_specs=[whole(s.shape) for s in out_shapes],
        ),
        out_shape=out_shapes,
        name="middle",
    )(
        own_depth.astype(jnp.int32)[None], parts, features, self_weight, other_ws, neigh_weight,
        other_wn, own_bias, other_bias, cotangent, other_cot,
    )
    out_received = lax.ppermute(out_other, "depth", swap)
    gw = gw_own + lax.ppermute(gw_other, "depth", swap)
    blocks = half // 128
    q_all = lax.all_to_all(
        jnp.broadcast_to(q[None], (plane, blocks, 128, 128)), ("col", "depth"), 0, 0, tiled=True
    ).reshape(plane * blocks, 128, 128)
    col_blocks = span * row_count // 128
    grad_partial = pl.pallas_call(
        backward_kernel,
        in_specs=[smem] * 3 + [vmem, hbm],
        out_specs=vmem,
        out_shape=jax.ShapeDtypeStruct((col_blocks, 128, 128), BF16),
        scratch_shapes=[scratch_tiles, pltpu.VMEM((col_blocks, 128, 128), F32), tile_sems],
        name="backward",
    )(info, rows, cols, q_all, tile_values)
    ring = row_count * depth_count
    grad_parts = lax.all_to_all(
        grad_partial.reshape(ring, blocks, 128, 128), ("row", "depth"), 0, 0, tiled=True
    )
    grad_features = pl.pallas_call(
        finish_kernel,
        in_specs=[vmem, vmem],
        out_specs=vmem,
        out_shape=jax.ShapeDtypeStruct((half, 128), BF16),
        name="finish",
    )(grad_parts, own_term)

    packed = jnp.concatenate(
        [
            gw[:256].reshape(col_count, 256 // col_count, 128),
            jnp.broadcast_to(gw[256:][None], (col_count, 8, 128)),
        ],
        axis=1,
    )
    piece = jnp.sum(lax.all_to_all(packed, "col", 0, 0, tiled=True), axis=0)
    piece = piece + sum(
        lax.ppermute(piece, "row", [(i, (i + k) % row_count) for i in range(row_count)])
        for k in range(1, row_count)
    )
    grad_scale = 1.0 / jnp.sqrt(jnp.float32(span * row_count * col_count))
    piece = piece * grad_scale
    rows_each = 256 // col_count
    full = lax.all_to_all(
        jnp.broadcast_to(piece[:rows_each][None], (col_count, rows_each, 128)),
        "col", 0, 0, tiled=True,
    ).reshape(256, 128)
    first = jnp.where(own_depth == 0, out_own, out_received)
    second = jnp.where(own_depth == 0, out_received, out_own)
    output = jnp.concatenate([first, second], axis=0)
    return (output, grad_features, full[:128], full[128:], piece[rows_each])


def solution(mesh):
    placed = (
        P(("row", "col"), None),
        P(None, "depth"),
        P(None, "depth"),
        P("depth"),
        P(("row", "col"), "depth"),
        P(("row", "col", "depth"), None, None),
        P(("row", "col", "depth"), None),
        P(("row", "col", "depth"), None),
        P(("row", "col", "depth")),
    )
    return jax.shard_map(
        body,
        mesh=mesh,
        in_specs=placed,
        out_specs=(
            P(("row", "col"), "depth"),
            P(("row", "col", "depth"), None),
            P(None, "depth"),
            P(None, "depth"),
            P("depth"),
        ),
        check_vma=False,
    )
```

time: 1040 us -> 163 us (0.16)
  waiting for transfers between devices: 623 us -> 67.7 us
  other arithmetic: 137 us -> 2.26 us
  blocking collectives: 134 us -> 10.5 us
  matrix products: 76.3 us -> 0 us
  starting transfers between devices: 0.32 us -> 57.9 us
  local copies, waits for them, and re-layouts: 48.7 us -> 7.43 us
  Pallas kernels: 0 us -> 14.4 us
  between operations: 14.9 us -> 1.51 us
    psum x1 -> x0, waiting for transfers between devices: 356 us -> none  [body(): lax.psum((self_local, neigh_local, bias_local), ('row', 'col'))]
    reduce_scatter x5 -> x0, waiting for transfers between devices: 205 us -> none  [the longest x1 95.5 us: body(): lax.psum_scatter(partial_value, 'col', scatter_dimension=0, tiled=True)]
    scatter-add x16 -> x0, other arithmetic: 132 us -> none  [add_group(): return totals.at[target].add(product)]
    psum x1 -> x0, blocking collectives: 119 us -> none  [body(): lax.psum((self_local, neigh_local, bias_local), ('row', 'col'))]
    dot_general x22 -> x0, matrix products: 76.3 us -> none  [the longest x8 37.8 us: add_group(): jnp.einsum('tij,tih->tjh', tile_block, source_blocks[out_index], preferre...]
    all_gather x2 -> x0, waiting for transfers between devices: 60.9 us -> none  [the longest x1 35.6 us: body(): grad_rows = lax.all_gather(grad_rows, 'col', axis=0, tiled=True)]
    gather x16 -> x0, local copies, waits for them, and re-layouts: 39.4 us -> none  [the longest x8 33.9 us: add_group(): source_blocks[out_index]]
    all_to_all x0 -> x4, starting transfers between devices: none -> 39 us  [the longest x1 17 us: body(): lax.all_to_all(partial.reshape(plane, half, 128), ('col', 'depth'), 0, 0,...]
  transfers between devices with their start and end apart: 8 -> 16, of which waited for: 8 -> 8; matrix products, arithmetic and copies ran while one was open for 1% -> 2% of each run, Pallas kernels for 0% -> 3%
where the time goes in v1:
time: 163 us; the launch traced here: 162 us
  waiting for transfers between devices  67.7 us (42%)
  starting transfers between devices  57.9 us (36%)
  Pallas kernels  14.4 us (9%)
  blocking collectives  10.5 us (6%)
  local copies, waits for them, and re-layouts  7.43 us (5%)
  other arithmetic  2.26 us (1%)
    ppermute x1, waiting for transfers between devices, body(): other_bias = lax.ppermute(own_bias, 'depth', swap)  23.4 us
    all_to_all x1, waiting for transfers between devices, body(): lax.all_to_all(jnp.broadcast_to(q[None], (plane, blocks, 128, 128)), ('co...  21.4 us
    all_to_all x1, starting transfers between devices, body(): lax.all_to_all(partial.reshape(plane, half, 128), ('col', 'depth'), 0, 0,...  17 us
    all_to_all x1, blocking collectives, body(): piece = jnp.sum(lax.all_to_all(packed, 'col', 0, 0, tiled=True), axis=0)  10.5 us
    all_to_all x1, waiting for transfers between devices, body(): lax.all_to_all(grad_partial.reshape(ring, blocks, 128, 128), ('row', 'dep...  10.1 us
    all_to_all x1, starting transfers between devices, body(): lax.all_to_all(grad_partial.reshape(ring, blocks, 128, 128), ('row', 'dep...  8.97 us
    all_to_all x1, starting transfers between devices, body(): lax.all_to_all(jnp.broadcast_to(piece[:rows_each][None], (col_count, rows...  6.84 us
    ppermute x3, waiting for transfers between devices, from_row(): lax.ppermute(features, 'row', [(i, (i + k) % row_count) for i in range(ro...  6.61 us
  transfers between devices with their start and end apart: 16, of which 8 were waited for; matrix products, arithmetic and copies ran while one was open for 2% of the time, Pallas kernels for 3%

profile of v1, /device:TPU:4, one launch (start us, length us, event | category | flops | bytes accessed | tf_op | source)
XLA Modules:
  0.0 161.7 jit_solution(8327582086818051926)
XLA Ops:
  0.6 3.1 %collective-permute-start.2 = (bf16[512,128]{1,0:T(8,128)(2,1)}, bf16[512,128]{1,0:T(8,128)(2,1)S(1)}, u32[]{:S(2)}, u32[]{:S(2)}) collective-permute-start(bf16[512,128]{1,0:T(8,128)(2,1)} %x.1), channel_id=1, source_target_pairs={{0,96},{32,0},{64,32},{96,64},{1,97},{33,1},{65,33},{97,65},{2,98}... | collective-permute-start | bytes 393224 | tf_op jit(solution)/shard_map/ppermute | solution.py:154
  6.6 3.0 %collective-permute-done.2.x3 = bf16[512,128]{1,0:T(8,128)(2,1)S(1)} collective-permute-done((bf16[512,128]{1,0:T(8,128)(2,1)}, bf16[512,128]{1,0:T(8,128)(2,1)S(1)}, u32[]{:S(2)}, u32[]{:S(2)}) %collective-permute-start.2) | collective-permute-done | bytes 131104 | tf_op jit(solution)/shard_map/ppermute | solution.py:154
  9.6 2.2 %collective-permute-done.1.x2 = bf16[512,128]{1,0:T(8,128)(2,1)S(1)} collective-permute-done((bf16[512,128]{1,0:T(8,128)(2,1)}, bf16[512,128]{1,0:T(8,128)(2,1)S(1)}, u32[]{:S(2)}, u32[]{:S(2)}) %collective-permute-start.1) | collective-permute-done | bytes 131104 | tf_op jit(solution)/shard_map/ppermute | solution.py:154
  11.8 1.4 collective-permute-done.x1
  13.9 4.7 %forward.1 = bf16[8192,128]{1,0:T(8,128)(2,1)} custom-call(s32[2]{0:T(128)} %pad_add_fusion.info, s32[256]{0:T(256)} %bitcast.19, s32[256]{0:T(256)} %bitcast.21, bf16[512,128]{1,0:T(8,128)(2,1)} %x.1, bf16[512,128]{1,0:T(8,128)(2,1)} %copy-done.6, bf16[512,128]{1,0:T(8,128)(2,1)} %copy-done.5, bf16[512,128]{1,0:T(8,128)(2,1)} %copy-done.4, ...), custom_call_target="tpu_custom_call" | custom-call | tf_op jit(solution)/shard_map/forward/pallas_call | solution.py:169
  18.6 17.0 %all-to-all-start = ((bf16[32,256,128]{2,1,0:T(8,128)(2,1)}), bf16[32,256,128]{2,1,0:T(8,128)(2,1)S(1)}, u32[]{:S(2)}, u32[]{:S(2)}) async-start(bf16[32,256,128]{2,1,0:T(8,128)(2,1)} %bitcast.14), calls=%async_computation | async-start | bytes 4194304 | tf_op jit(solution)/shard_map/all_to_all | solution.py:184
  35.6 3.0 %collective-permute-start.6 = (bf16[256,128]{1,0:T(8,128)(2,1)S(1)}, bf16[256,128]{1,0:T(8,128)(2,1)S(1)}, u32[]{:S(2)}, u32[]{:S(2)}) collective-permute-start(bf16[256,128]{1,0:T(8,128)(2,1)S(1)} %constant_dynamic-slice_fusion), channel_id=1, source_target_pairs={{0,1},{1,0},{2,3},{3,2},{4,5},{5,4},{6,7},{7,6},{8,9},{9,8},{10,11... | collective-permute-start | bytes 196616 | tf_op jit(solution)/shard_map/ppermute | solution.py:157
  39.2 3.0 %collective-permute-start.4 = (bf16[128,128]{1,0:T(8,128)(2,1)S(1)}, bf16[128,128]{1,0:T(8,128)(2,1)S(1)}, u32[]{:S(2)}, u32[]{:S(2)}) collective-permute-start(bf16[128,128]{1,0:T(8,128)(2,1)S(1)} %copy-done.10), channel_id=1, source_target_pairs={{0,1},{1,0},{2,3},{3,2},{4,5},{5,4},{6,7},{7,6},{8,9},{9,8},{10,11... | collective-permute-start | bytes 98312 | tf_op jit(solution)/shard_map/ppermute | solution.py:161
  42.7 23.4 %collective-permute-done.5.b_b = f32[1,128]{1,0:T(1,128)S(1)} collective-permute-done((f32[1,128]{1,0:T(1,128)S(1)}, f32[1,128]{1,0:T(1,128)S(1)}, u32[]{:S(2)}, u32[]{:S(2)}) %collective-permute-start.5) | collective-permute-done | bytes 544 | tf_op jit(solution)/shard_map/ppermute | solution.py:163
  67.5 3.3 %middle.1 = (bf16[256,128]{1,0:T(8,128)(2,1)}, bf16[256,128]{1,0:T(8,128)(2,1)}, bf16[2,128,128]{2,1,0:T(8,128)(2,1)}, f32[256,128]{1,0:T(8,128)}, f32[264,128]{1,0:T(8,128)}, /*index=5*/f32[264,128]{1,0:T(8,128)}) custom-call(s32[1]{0:T(128)} %bitcast.depth, bf16[32,256,128]{2,1,0:T(8,128)(2,1)} %copy-done, bf16[512,128]{1,0:T(8,128)(2,1)} %x.1, ...), custom_call_target="tpu_custom_call" | custom-call | tf_op jit(solution)/shard_map/middle/pallas_call | solution.py:202
  70.8 1.9 %collective-permute-start.8 = (f32[264,128]{1,0:T(8,128)}, f32[264,128]{1,0:T(8,128)S(1)}, u32[]{:S(2)}, u32[]{:S(2)}) collective-permute-start(f32[264,128]{1,0:T(8,128)} %get-tuple-element.16), channel_id=1, source_target_pairs={{0,1},{1,0},{2,3},{3,2},{4,5},{5,4},{6,7},{7,6},{8,9},{9,8},{10,11... | collective-permute-start | bytes 405512 | tf_op jit(solution)/shard_map/ppermute | solution.py:223
  72.6 4.9 %collective-permute-done.8 = f32[264,128]{1,0:T(8,128)S(1)} collective-permute-done((f32[264,128]{1,0:T(8,128)}, f32[264,128]{1,0:T(8,128)S(1)}, u32[]{:S(2)}, u32[]{:S(2)}) %collective-permute-start.8) | collective-permute-done | bytes 135200 | tf_op jit(solution)/shard_map/ppermute | solution.py:223
  78.5 10.5 %all_to_all.25 = f32[16,24,128]{2,1,0:T(8,128)S(1)} all-to-all(f32[16,24,128]{2,1,0:T(8,128)S(1)} %pad_maximum_fusion), channel_id=1, replica_groups=mesh['row'=4,'col'=16,'depth'=2] {'col'}, dimensions={0} | all-to-all | bytes 393216 | tf_op jit(solution)/shard_map/all_to_all | solution.py:256
  89.0 2.7 %broadcast_in_dim.12 = bf16[32,2,128,128]{3,2,1,0:T(8,128)(2,1)} broadcast(bf16[2,128,128]{2,1,0:T(8,128)(2,1)} %get-tuple-element.13), dimensions={1,2,3} | broadcast | bytes 2162688 | tf_op jit(solution)/shard_map/broadcast_in_dim | solution.py:226
  91.7 6.2 %all-to-all-start.1 = ((bf16[32,2,128,128]{3,2,1,0:T(8,128)(2,1)}), bf16[32,2,128,128]{3,2,1,0:T(8,128)(2,1)S(1)}, u32[]{:S(2)}, u32[]{:S(2)}) async-start(bf16[32,2,128,128]{3,2,1,0:T(8,128)(2,1)} %broadcast_in_dim.12), calls=%async_computation.1 | async-start | bytes 4194304 | tf_op jit(solution)/shard_map/all_to_all | solution.py:225
  98.0 1.2 collective-permute-start.11
  100.2 3.0 %collective-permute-start.7 = (bf16[256,128]{1,0:T(8,128)(2,1)S(1)}, bf16[256,128]{1,0:T(8,128)(2,1)S(1)}, u32[]{:S(2)}, u32[]{:S(2)}) collective-permute-start(bf16[256,128]{1,0:T(8,128)(2,1)S(1)} %copy-done.15), channel_id=1, source_target_pairs={{0,1},{1,0},{2,3},{3,2},{4,5},{5,4},{6,7},{7,6},{8,9},{9,8},{10,11... | collective-permute-start | bytes 196616 | tf_op jit(solution)/shard_map/ppermute | solution.py:222
  103.1 1.3 collective-permute-done.10
  104.5 21.4 %all-to-all-done.1 = bf16[32,2,128,128]{3,2,1,0:T(8,128)(2,1)S(1)} async-done(((bf16[32,2,128,128]{3,2,1,0:T(8,128)(2,1)}), bf16[32,2,128,128]{3,2,1,0:T(8,128)(2,1)S(1)}, u32[]{:S(2)}, u32[]{:S(2)}) %all-to-all-start.1) | async-done | bytes 2097184 | tf_op jit(solution)/shard_map/all_to_all | solution.py:225
  126.6 6.8 %all-to-all-start.4 = ((f32[16,16,128]{2,1,0:T(8,128)}), f32[16,16,128]{2,1,0:T(8,128)S(1)}, u32[]{:S(2)}, u32[]{:S(2)}) async-start(f32[16,16,128]{2,1,0:T(8,128)} %broadcast_in_dim.28), calls=%async_computation.4 | async-start | bytes 262144 | tf_op jit(solution)/shard_map/all_to_all | solution.py:264
  133.5 4.7 %backward.1 = bf16[16,128,128]{2,1,0:T(8,128)(2,1)} custom-call(s32[2]{0:T(128)} %pad_add_fusion.info, s32[256]{0:T(256)} %bitcast.20, s32[256]{0:T(256)} %bitcast.22, bf16[64,128,128]{2,1,0:T(8,128)(2,1)} %bitcast.13, bf16[256,128,128]{2,1,0:T(8,128)(2,1)} %tiles.3), custom_call_target="tpu_custom_call" | custom-call | tf_op jit(solution)/shard_map/backward/pallas_call | solution.py:229
  138.2 9.0 %all-to-all-start.2 = ((bf16[8,2,128,128]{3,2,1,0:T(8,128)(2,1)}), bf16[8,2,128,128]{3,2,1,0:T(8,128)(2,1)S(1)}, u32[]{:S(2)}, u32[]{:S(2)}) async-start(bf16[8,2,128,128]{3,2,1,0:T(8,128)(2,1)} %bitcast.15), calls=%async_computation.2 | async-start | bytes 1048576 | tf_op jit(solution)/shard_map/all_to_all | solution.py:238
  149.0 10.1 %all-to-all-done.2.parts = bf16[8,2,128,128]{3,2,1,0:T(8,128)(2,1)S(1)} async-done(((bf16[8,2,128,128]{3,2,1,0:T(8,128)(2,1)}), bf16[8,2,128,128]{3,2,1,0:T(8,128)(2,1)S(1)}, u32[]{:S(2)}, u32[]{:S(2)}) %all-to-all-start.2) | async-done | bytes 524320 | tf_op jit(solution)/shard_map/all_to_all | solution.py:238
  159.9 1.8 %finish.1 = bf16[256,128]{1,0:T(8,128)(2,1)} custom-call(bf16[8,2,128,128]{3,2,1,0:T(8,128)(2,1)} %copy-done.2, f32[256,128]{1,0:T(8,128)} %get-tuple-element.14.own_term), custom_call_target="tpu_custom_call" | custom-call | tf_op jit(solution)/shard_map/finish/pallas_call | solution.py:241
  (61 shorter events, 10.7 us)
Async XLA Ops:
  0.6 9.0 %collective-permute-start.2 = (bf16[512,128]{1,0:T(8,128)(2,1)}, bf16[512,128]{1,0:T(8,128)(2,1)S(1)}, u32[]{:S(2)}, u32[]{:S(2)}) collective-permute-start(bf16[512,128]{1,0:T(8,128)(2,1)} %x.1), channel_id=1, source_target_pairs={{0,96},{32,0},{64,32},{96,64},{1,97},{33,1},{65,33},{97,65},{2,98}... | collective-permute-start | bytes 393224 | tf_op jit(solution)/shard_map/ppermute | solution.py:154
  3.7 8.1 %collective-permute-start.1 = (bf16[512,128]{1,0:T(8,128)(2,1)}, bf16[512,128]{1,0:T(8,128)(2,1)S(1)}, u32[]{:S(2)}, u32[]{:S(2)}) collective-permute-start(bf16[512,128]{1,0:T(8,128)(2,1)} %x.1), channel_id=1, source_target_pairs={{0,64},{32,96},{64,0},{96,32},{1,65},{33,97},{65,1},{97,33},{2,66}... | collective-permute-start | bytes 393224 | tf_op jit(solution)/shard_map/ppermute | solution.py:154
  4.3 8.9 %collective-permute-start = (bf16[512,128]{1,0:T(8,128)(2,1)}, bf16[512,128]{1,0:T(8,128)(2,1)S(1)}, u32[]{:S(2)}, u32[]{:S(2)}) collective-permute-start(bf16[512,128]{1,0:T(8,128)(2,1)} %x.1), channel_id=1, source_target_pairs={{0,32},{32,64},{64,96},{96,0},{1,33},{33,65},{65,97},{97,1},{2,34}... | collective-permute-start | bytes 393224 | tf_op jit(solution)/shard_map/ppermute | solution.py:154
  9.6 3.6 %copy-start.4 = (bf16[512,128]{1,0:T(8,128)(2,1)}, bf16[512,128]{1,0:T(8,128)(2,1)S(1)}, u32[]{:S(2)}) copy-start(bf16[512,128]{1,0:T(8,128)(2,1)S(1)} %collective-permute-done.2.x3) | copy-start | bytes 393220
  18.5 17.0 %copy-start.3 = (bf16[512,128]{1,0:T(8,128)(2,1)S(1)}, bf16[512,128]{1,0:T(8,128)(2,1)}, u32[]{:S(2)}) copy-start(bf16[512,128]{1,0:T(8,128)(2,1)} %cot_a.1) | copy-start | bytes 393220
  18.5 20.1 %copy-start.9 = (bf16[128,128]{1,0:T(8,128)(2,1)S(1)}, bf16[128,128]{1,0:T(8,128)(2,1)}, u32[]{:S(2)}) copy-start(bf16[128,128]{1,0:T(8,128)(2,1)} %ws_a.1) | copy-start | bytes 98308
  18.6 20.6 %copy-start.10 = (bf16[128,128]{1,0:T(8,128)(2,1)S(1)}, bf16[128,128]{1,0:T(8,128)(2,1)}, u32[]{:S(2)}) copy-start(bf16[128,128]{1,0:T(8,128)(2,1)} %wn_a.1) | copy-start | bytes 98308
  18.6 23.6 %copy-start.13 = (f32[128]{0:T(128)S(1)}, f32[128]{0:T(128)}, u32[]{:S(2)}) copy-start(f32[128]{0:T(128)} %param.12) | copy-start | bytes 1540
  18.6 47.6 %all-to-all-start = ((bf16[32,256,128]{2,1,0:T(8,128)(2,1)}), bf16[32,256,128]{2,1,0:T(8,128)(2,1)S(1)}, u32[]{:S(2)}, u32[]{:S(2)}) async-start(bf16[32,256,128]{2,1,0:T(8,128)(2,1)} %bitcast.14), calls=%async_computation | async-start | bytes 4194304 | tf_op jit(solution)/shard_map/all_to_all | solution.py:184
  35.6 30.6 %collective-permute-start.6 = (bf16[256,128]{1,0:T(8,128)(2,1)S(1)}, bf16[256,128]{1,0:T(8,128)(2,1)S(1)}, u32[]{:S(2)}, u32[]{:S(2)}) collective-permute-start(bf16[256,128]{1,0:T(8,128)(2,1)S(1)} %constant_dynamic-slice_fusion), channel_id=1, source_target_pairs={{0,1},{1,0},{2,3},{3,2},{4,5},{5,4},{6,7},{7,6},{8,9},{9,8},{10,11... | collective-permute-start | bytes 196616 | tf_op jit(solution)/shard_map/ppermute | solution.py:157
  38.6 27.5 %collective-permute-start.3 = (bf16[128,128]{1,0:T(8,128)(2,1)S(1)}, bf16[128,128]{1,0:T(8,128)(2,1)S(1)}, u32[]{:S(2)}, u32[]{:S(2)}) collective-permute-start(bf16[128,128]{1,0:T(8,128)(2,1)S(1)} %copy-done.9), channel_id=1, source_target_pairs={{0,1},{1,0},{2,3},{3,2},{4,5},{5,4},{6,7},{7,6},{8,9},{9,8},{10,11... | collective-permute-start | bytes 98312 | tf_op jit(solution)/shard_map/ppermute | solution.py:160
  39.2 26.9 %collective-permute-start.4 = (bf16[128,128]{1,0:T(8,128)(2,1)S(1)}, bf16[128,128]{1,0:T(8,128)(2,1)S(1)}, u32[]{:S(2)}, u32[]{:S(2)}) collective-permute-start(bf16[128,128]{1,0:T(8,128)(2,1)S(1)} %copy-done.10), channel_id=1, source_target_pairs={{0,1},{1,0},{2,3},{3,2},{4,5},{5,4},{6,7},{7,6},{8,9},{9,8},{10,11... | collective-permute-start | bytes 98312 | tf_op jit(solution)/shard_map/ppermute | solution.py:161
  42.2 24.0 %collective-permute-start.5 = (f32[1,128]{1,0:T(1,128)S(1)}, f32[1,128]{1,0:T(1,128)S(1)}, u32[]{:S(2)}, u32[]{:S(2)}) collective-permute-start(f32[1,128]{1,0:T(1,128)S(1)} %bitcast.24), channel_id=1, source_target_pairs={{0,1},{1,0},{2,3},{3,2},{4,5},{5,4},{6,7},{7,6},{8,9},{9,8},{10,11... | collective-permute-start | bytes 1544 | tf_op jit(solution)/shard_map/ppermute | solution.py:163
  70.8 6.7 %collective-permute-start.8 = (f32[264,128]{1,0:T(8,128)}, f32[264,128]{1,0:T(8,128)S(1)}, u32[]{:S(2)}, u32[]{:S(2)}) collective-permute-start(f32[264,128]{1,0:T(8,128)} %get-tuple-element.16), channel_id=1, source_target_pairs={{0,1},{1,0},{2,3},{3,2},{4,5},{5,4},{6,7},{7,6},{8,9},{9,8},{10,11... | collective-permute-start | bytes 405512 | tf_op jit(solution)/shard_map/ppermute | solution.py:223
  91.7 8.5 %copy-start.15 = (bf16[256,128]{1,0:T(8,128)(2,1)S(1)}, bf16[256,128]{1,0:T(8,128)(2,1)}, u32[]{:S(2)}) copy-start(bf16[256,128]{1,0:T(8,128)(2,1)} %get-tuple-element.12) | copy-start | bytes 196612
  91.7 41.8 %copy-start.7 = (bf16[256,128]{1,0:T(8,128)(2,1)S(1)}, bf16[256,128]{1,0:T(8,128)(2,1)}, u32[]{:S(2)}) copy-start(bf16[256,128]{1,0:T(8,128)(2,1)} %get-tuple-element.11) | copy-start | bytes 196612
  91.7 34.2 %all-to-all-start.1 = ((bf16[32,2,128,128]{3,2,1,0:T(8,128)(2,1)}), bf16[32,2,128,128]{3,2,1,0:T(8,128)(2,1)S(1)}, u32[]{:S(2)}, u32[]{:S(2)}) async-start(bf16[32,2,128,128]{3,2,1,0:T(8,128)(2,1)} %broadcast_in_dim.12), calls=%async_computation.1 | async-start | bytes 4194304 | tf_op jit(solution)/shard_map/all_to_all | solution.py:225
  98.0 5.2 %collective-permute-start.11 = (f32[24,128]{1,0:T(8,128)S(1)}, f32[24,128]{1,0:T(8,128)S(1)}, u32[]{:S(2)}, u32[]{:S(2)}) collective-permute-start(f32[24,128]{1,0:T(8,128)S(1)} %reduce_sum.9), channel_id=1, source_target_pairs={{0,96},{32,0},{64,32},{96,64},{1,97},{33,1},{65,33},{97,65},{2,98}... | collective-permute-start | bytes 36872 | tf_op jit(solution)/shard_map/ppermute | solution.py:258
  99.2 5.3 %collective-permute-start.10 = (f32[24,128]{1,0:T(8,128)S(1)}, f32[24,128]{1,0:T(8,128)S(1)}, u32[]{:S(2)}, u32[]{:S(2)}) collective-permute-start(f32[24,128]{1,0:T(8,128)S(1)} %reduce_sum.9), channel_id=1, source_target_pairs={{0,64},{32,96},{64,0},{96,32},{1,65},{33,97},{65,1},{97,33},{2,66}... | collective-permute-start | bytes 36872 | tf_op jit(solution)/shard_map/ppermute | solution.py:258
  99.2 5.3 %collective-permute-start.9 = (f32[24,128]{1,0:T(8,128)S(1)}, f32[24,128]{1,0:T(8,128)S(1)}, u32[]{:S(2)}, u32[]{:S(2)}) collective-permute-start(f32[24,128]{1,0:T(8,128)S(1)} %reduce_sum.9), channel_id=1, source_target_pairs={{0,32},{32,64},{64,96},{96,0},{1,33},{33,65},{65,97},{97,1},{2,34}... | collective-permute-start | bytes 36872 | tf_op jit(solution)/shard_map/ppermute | solution.py:258
  100.2 33.3 %collective-permute-start.7 = (bf16[256,128]{1,0:T(8,128)(2,1)S(1)}, bf16[256,128]{1,0:T(8,128)(2,1)S(1)}, u32[]{:S(2)}, u32[]{:S(2)}) collective-permute-start(bf16[256,128]{1,0:T(8,128)(2,1)S(1)} %copy-done.15), channel_id=1, source_target_pairs={{0,1},{1,0},{2,3},{3,2},{4,5},{5,4},{6,7},{7,6},{8,9},{9,8},{10,11... | collective-permute-start | bytes 196616 | tf_op jit(solution)/shard_map/ppermute | solution.py:222
  125.9 7.6 %copy-start.1 = (bf16[32,2,128,128]{3,2,1,0:T(8,128)(2,1)}, bf16[32,2,128,128]{3,2,1,0:T(8,128)(2,1)S(1)}, u32[]{:S(2)}) copy-start(bf16[32,2,128,128]{3,2,1,0:T(8,128)(2,1)S(1)} %all-to-all-done.1) | copy-start | bytes 6291460
  126.6 11.6 %all-to-all-start.4 = ((f32[16,16,128]{2,1,0:T(8,128)}), f32[16,16,128]{2,1,0:T(8,128)S(1)}, u32[]{:S(2)}, u32[]{:S(2)}) async-start(f32[16,16,128]{2,1,0:T(8,128)} %broadcast_in_dim.28), calls=%async_computation.4 | async-start | bytes 262144 | tf_op jit(solution)/shard_map/all_to_all | solution.py:264
  138.2 20.9 %all-to-all-start.2 = ((bf16[8,2,128,128]{3,2,1,0:T(8,128)(2,1)}), bf16[8,2,128,128]{3,2,1,0:T(8,128)(2,1)S(1)}, u32[]{:S(2)}, u32[]{:S(2)}) async-start(bf16[8,2,128,128]{3,2,1,0:T(8,128)(2,1)} %bitcast.15), calls=%async_computation.2 | async-start | bytes 1048576 | tf_op jit(solution)/shard_map/all_to_all | solution.py:238
  (8 other events, 6.7 us)

commit v2 on v1

v2 whole, which is shorter than its diff:
```python
import jax
import jax.numpy as jnp
from jax import lax
from jax.experimental import pallas as pl
from jax.experimental.pallas import tpu as pltpu
from jax.sharding import Mesh, PartitionSpec as P


GROUP = 32
F32 = jnp.float32
BF16 = jnp.bfloat16


def dot_nn(a, b):
    return lax.dot_general(a, b, (((1,), (0,)), ((), ())), preferred_element_type=F32)


def dot_nt(a, b):
    return lax.dot_general(a, b, (((1,), (1,)), ((), ())), preferred_element_type=F32)


def dot_tn(a, b):
    return lax.dot_general(a, b, (((0,), (0,)), ((), ())), preferred_element_type=F32)


def tile_copy(group, tiles, tile_buf, sems):
    at = pl.ds(group * GROUP, GROUP)
    return pltpu.make_async_copy(tiles.at[at], tile_buf.at[at], sems.at[group])


def start_tiles(live_groups, tiles, tile_buf, sems):
    def start(group, carry):
        tile_copy(group, tiles, tile_buf, sems).start()
        return carry

    lax.fori_loop(0, live_groups, start, 0)


def for_tiles(live_groups, tiles, tile_buf, sems, step):
    def one_group(group, carry):
        tile_copy(group, tiles, tile_buf, sems).wait()
        for k in range(GROUP):
            step(group * GROUP + k)
        return carry

    lax.fori_loop(0, live_groups, one_group, 0)


def forward_kernel(
    live, into, source, x0, x1, x2, x3, tiles, acc, other, x_buf, tile_buf, sems, x_sems
):
    live_groups = live[0] // GROUP
    start_tiles(live_groups, tiles, tile_buf, sems)
    span = x0.shape[0]
    copies = [
        pltpu.make_async_copy(shard, x_buf.at[pl.ds(k * span, span)], x_sems.at[k])
        for k, shard in enumerate((x0, x1, x2, x3))
    ]
    for copy in copies:
        copy.start()
    acc[...] = jnp.zeros_like(acc)
    for copy in copies:
        copy.wait()

    def step(t):
        block = x_buf[pl.ds(pl.multiple_of(source[t] * 128, 128), 128), :]
        target = pl.ds(pl.multiple_of(into[t] * 128, 128), 128)
        acc[target, :] += dot_nn(tile_buf[t], block)

    for_tiles(live_groups, tiles, tile_buf, sems, step)
    other[...] = acc[other.shape[0] :, :].astype(BF16)


def backward_kernel(live, into, cols, q_own, q_other, tiles, out, q_buf, tile_buf, acc, sems, q_sems):
    live_groups = live[0] // GROUP
    start_tiles(live_groups, tiles, tile_buf, sems)
    half = q_own.shape[0]
    copies = [
        pltpu.make_async_copy(part, q_buf.at[pl.ds(k * half, half)], q_sems.at[k])
        for k, part in enumerate((q_own, q_other))
    ]
    for copy in copies:
        copy.start()
    acc[...] = jnp.zeros_like(acc)
    for copy in copies:
        copy.wait()

    def step(t):
        acc[cols[t]] += dot_nn(q_buf[into[t]], tile_buf[t])

    for_tiles(live_groups, tiles, tile_buf, sems, step)
    out[...] = acc[...].astype(BF16)


def pack_kernel(cot, ws, wn, bias, packed):
    half = cot.shape[0] // 2
    other = 1 - lax.axis_index("depth")
    packed[0:half] = cot[pl.ds(other * half, half), :]
    packed[half : half + 128] = ws[...]
    packed[half + 128 : half + 256] = wn[...]
    first = bias[...].astype(BF16)
    rest = bias[...] - first.astype(F32)
    second = rest.astype(BF16)
    third = (rest - second.astype(F32)).astype(BF16)
    row = lax.broadcasted_iota(jnp.int32, (16, 128), 0)
    lines = jnp.where(row == 0, first.astype(F32), jnp.where(row == 1, second.astype(F32), third.astype(F32)))
    packed[half + 256 : half + 272] = jnp.where(row < 3, lines, 0.0).astype(BF16)


def own_part(ref):
    half = ref.shape[0] // 2
    return ref[pl.ds(lax.axis_index("depth") * half, half), :]


def middle_kernel(
    parts, x, ws_a, wn_a, b_a, cot_a, packed, out_a, out_b, q, g_a, g_b, high_out, low_out
):
    total = parts[0].astype(F32)
    for k in range(1, parts.shape[0]):
        total = total + parts[k].astype(F32)
    high = total.astype(BF16)
    low = (total - high.astype(F32)).astype(BF16)
    high_out[...] = high
    low_out[...] = low
    x_val = own_part(x)
    half = x_val.shape[0]
    ws_b = packed[half : half + 128]
    wn_b = packed[half + 128 : half + 256]
    b_b = jnp.sum(packed[half + 256 : half + 272].astype(F32), axis=0, keepdims=True)
    for ws, wn, b, cot, out, g in (
        (ws_a[...], wn_a[...], b_a[...], own_part(cot_a), out_a, g_a),
        (ws_b, wn_b, b_b, packed[0:half], out_b, g_b),
    ):
        pre = dot_nn(x_val, ws) + (dot_nn(high, wn) + dot_nn(low, wn)) + b
        gate = jax.nn.sigmoid(pre)
        out[...] = (pre * gate).astype(BF16)
        g[...] = (cot.astype(F32) * gate * (1.0 + pre * (1.0 - gate))).astype(BF16)
    for k in range(q.shape[1]):
        at = slice(k * 128, (k + 1) * 128)
        block = (dot_nt(wn_a[...], g_a[at]) + dot_nt(wn_b, g_b[at])).astype(BF16)
        for copy in range(q.shape[0]):
            q[copy, k] = block


def weights_kernel(x, ws_a, packed, g_a, g_b, high, low, own_term, keep, send):
    x_val = own_part(x)
    half = x_val.shape[0]
    ws_b = packed[half : half + 128]
    own_term[...] = dot_nt(g_a[...], ws_a[...]) + dot_nt(g_b[...], ws_b)

    def fill(first, second):
        for k, g_ref in enumerate((g_a, g_b)):
            g = g_ref[...]
            first[k, 0:128] = dot_tn(x_val, g)
            second[k, 0:128] = dot_tn(high[...], g) + dot_tn(low[...], g)
            line = jnp.broadcast_to(jnp.sum(g.astype(F32), axis=0, keepdims=True), (8, 128))
            first[k, 128:136] = line
            second[k, 128:136] = line

    @pl.when(lax.axis_index("core") == 0)
    def _():
        fill(keep, send)

    @pl.when(lax.axis_index("core") == 1)
    def _():
        fill(send, keep)


def finish_kernel(parts, own_term, out):
    for k in range(parts.shape[1]):
        total = parts[0, k].astype(F32)
        for m in range(1, parts.shape[0]):
            total = total + parts[m, k].astype(F32)
        at = slice(k * 128, (k + 1) * 128)
        out[at] = (total.T + own_term[at]).astype(BF16)


def shift(value, axis, by):
    size = lax.axis_size(axis)
    return lax.ppermute(value, axis, [(i, (i + by) % size) for i in range(size)])


def sum_over(value, axis):
    size = lax.axis_size(axis)
    return value + sum(shift(value, axis, k) for k in range(1, size))


def body(
    features,
    self_weight,
    neigh_weight,
    bias,
    cotangent,
    tile_values,
    tile_rows,
    tile_cols,
    tile_counts,
):
    span = features.shape[0]
    half = span // 2
    blocks = half // 128
    slots = tile_values.shape[0]
    row_count = lax.axis_size("row")
    own_row = lax.axis_index("row")
    own_core = lax.axis_index("core")
    own_depth = lax.axis_index("depth")
    plane = ("depth", "near", "x")
    chips = lax.axis_size("x") * lax.axis_size("near") * lax.axis_size("depth")
    vmem = pl.BlockSpec(memory_space=pltpu.VMEM)
    smem = pl.BlockSpec(memory_space=pltpu.SMEM)
    hbm = pl.BlockSpec(memory_space=pl.ANY)
    scratch_tiles = pltpu.VMEM((slots, 128, 128), BF16)
    tile_sems = pltpu.SemaphoreType.DMA((slots // GROUP,))

    def in_vmem(value):
        return pltpu.with_memory_space_constraint(value, pltpu.VMEM)

    shards = [pltpu.with_memory_space_constraint(features, pltpu.HBM)] + [
        in_vmem(shift(features, "row", k)) for k in (2, 1, 3)
    ]
    own_bias = bias[None, :]
    packed = pl.pallas_call(
        pack_kernel,
        in_specs=[vmem] * 4,
        out_specs=vmem,
        out_shape=pltpu.VMEM((half + 272, 128), BF16),
        compiler_params=pltpu.CompilerParams(vmem_limit_bytes=4 * 1024 * 1024),
        name="pack",
    )(cotangent, self_weight, neigh_weight, own_bias)
    packed = shift(packed, "depth", 1)

    tiles = pltpu.with_memory_space_constraint(tile_values, pltpu.HBM)
    rows = tile_rows[0]
    cols = tile_cols[0]
    span_blocks = span // 128
    behind = (own_row - cols // span_blocks) % row_count
    source = jnp.where(behind == 1, 2, jnp.where(behind == 2, 1, behind)) * span_blocks
    source = source + cols % span_blocks
    owner = rows // blocks
    chip = owner % 2 * 8 + owner // 4 % 2 * 4 + owner // 8
    apart = (owner // 2 % 2) ^ own_core
    into = (apart * chips + chip) * blocks + rows % blocks
    half_rows = chips * half

    def build_shape(shape, dtype):
        return jax.ShapeDtypeStruct(shape, dtype)

    acc, other = pl.pallas_call(
        forward_kernel,
        in_specs=[smem] * 3 + [hbm] * 5,
        out_specs=[vmem, vmem],
        out_shape=[pltpu.VMEM((2 * half_rows, 128), F32), pltpu.VMEM((half_rows, 128), BF16)],
        scratch_shapes=[
            pltpu.VMEM((span * row_count, 128), BF16),
            scratch_tiles,
            tile_sems,
            pltpu.SemaphoreType.DMA((row_count,)),
        ],
        compiler_params=pltpu.CompilerParams(vmem_limit_bytes=16 * 1024 * 1024),
        name="forward",
    )(tile_counts, into, source, *shards, tiles)
    summed = (acc[:half_rows] + shift(other, "core", 1).astype(F32)).astype(BF16)
    parts = lax.all_to_all(summed.reshape(chips, half, 128), plane, 0, 0, tiled=True)
    parts = in_vmem(parts)

    def small_call(kernel, inputs, out_shape):
        return pl.pallas_call(
            kernel,
            in_specs=[vmem] * len(inputs),
            out_specs=[vmem] * len(out_shape),
            out_shape=out_shape,
            compiler_params=pltpu.CompilerParams(vmem_limit_bytes=12 * 1024 * 1024),
        )(*inputs)

    node_shape = build_shape((half, 128), BF16)
    out_own, out_other, q, g_a, g_b, high, low = small_call(
        middle_kernel,
        (parts, features, self_weight, neigh_weight, own_bias, cotangent, packed),
        [node_shape, node_shape, pltpu.VMEM((chips, blocks, 128, 128), BF16)] + [node_shape] * 4,
    )
    q_own = lax.all_to_all(q, plane, 0, 0, tiled=True).reshape(chips * blocks, 128, 128)
    q_own = in_vmem(q_own)
    gw_shape = build_shape((2, 136, 128), F32)
    own_term, keep, send = small_call(
        weights_kernel,
        (features, self_weight, packed, g_a, g_b, high, low),
        [build_shape((half, 128), F32), gw_shape, gw_shape],
    )
    out_received = shift(out_other, "depth", 1)
    gw = keep + shift(send, "core", 1)
    gw = sum_over(gw, "row")
    q_own, gw = lax.optimization_barrier((q_own, gw))
    q_other = in_vmem(shift(q_own, "core", 1))
    near = lax.axis_size("near")
    moves = [
        lax.ppermute(
            gw[flip],
            ("near", "depth"),
            [(n * 2 + d, (n ^ step) * 2 + (d ^ flip)) for n in range(near) for d in range(2)],
        )
        for step, flip in ((1, 0), (0, 1), (1, 1))
    ]
    gw = gw[0] + moves[0] + moves[1] + moves[2]
    gw = sum_over(gw, "x")
    col_blocks = span * row_count // 128
    grad_partial = pl.pallas_call(
        backward_kernel,
        in_specs=[smem] * 3 + [hbm] * 3,
        out_specs=vmem,
        out_shape=pltpu.VMEM((col_blocks, 128, 128), BF16),
        scratch_shapes=[
            pltpu.VMEM((2 * chips * blocks, 128, 128), BF16),
            scratch_tiles,
            pltpu.VMEM((col_blocks, 128, 128), F32),
            tile_sems,
            pltpu.SemaphoreType.DMA((2,)),
        ],
        compiler_params=pltpu.CompilerParams(vmem_limit_bytes=16 * 1024 * 1024),
        name="backward",
    )(tile_counts, into, cols, q_own, q_other, tiles)
    ring = row_count * 2
    grad_parts = in_vmem(
        lax.all_to_all(
            grad_partial.reshape(ring, blocks, 128, 128), ("row", "depth"), 0, 0, tiled=True
        )
    )
    grad_features = pl.pallas_call(
        finish_kernel,
        in_specs=[vmem, vmem],
        out_specs=vmem,
        out_shape=node_shape,
        compiler_params=pltpu.CompilerParams(vmem_limit_bytes=8 * 1024 * 1024),
        name="finish",
    )(grad_parts, own_term)

    gw = gw * (1.0 / jnp.sqrt(jnp.float32(span * row_count * 2 * chips // 2)))
    mine_gw = gw[:128]
    other_gw = shift(mine_gw, "core", 1)
    is_first = own_core == 0
    grad_self = jnp.where(is_first, mine_gw, other_gw)
    grad_neigh = jnp.where(is_first, other_gw, mine_gw)
    first = jnp.where(own_depth == 0, out_own, out_received)
    second = jnp.where(own_depth == 0, out_received, out_own)
    output = jnp.concatenate([first, second], axis=0)
    return (output, grad_features, grad_self, grad_neigh, gw[128])


def solution(mesh):
    fine = Mesh(mesh.devices.reshape(4, 4, 2, 2, 2), ("row", "x", "near", "core", "depth"))
    nodes = ("row", "x", "near", "core")
    every = nodes + ("depth",)
    placed = (
        P(nodes, None),
        P(None, "depth"),
        P(None, "depth"),
        P("depth"),
        P(nodes, "depth"),
        P(every, None, None),
        P(every, None),
        P(every, None),
        P(every),
    )

    return jax.shard_map(
        body,
        mesh=fine,
        in_specs=placed,
        out_specs=(P(nodes, "depth"), P(every, None), P(None, "depth"), P(None, "depth"), P("depth")),
        check_vma=False,
    )
```

time: 163 us -> 109 us (0.67)
  waiting for transfers between devices: 67.7 us -> 40.3 us
  blocking collectives: 10.5 us -> 0 us
  starting transfers between devices: 57.9 us -> 49.9 us
  local copies, waits for them, and re-layouts: 7.43 us -> 0.56 us
  Pallas kernels: 14.4 us -> 12.4 us
    all_to_all x3 -> x2, waiting for transfers between devices: 21.4 us -> 0.06 us  [the longest x1 0.06 us: body(): lax.all_to_all(q, plane, 0, 0, tiled=True).reshape(chips * blocks, 128, 128)]
    all_to_all x3 -> x2, starting transfers between devices: 30 us -> 15.9 us  [the longest x1 10.5 us: body(): lax.all_to_all(summed.reshape(chips, half, 128), plane, 0, 0, tiled=True)]
    all_to_all x1 -> x0, blocking collectives: 10.5 us -> none  [body(): piece = jnp.sum(lax.all_to_all(packed, 'col', 0, 0, tiled=True), axis=0)]
    ppermute x12 -> x18, starting transfers between devices: 18.9 us -> 26.1 us  [the longest x15 22.5 us: shift(): lax.ppermute(value, axis, [(i, (i + by) % size) for i in range(size)])]
    ppermute x12 -> x18, waiting for transfers between devices: 36.3 us -> 32.6 us  [the longest x15 28.6 us: shift(): lax.ppermute(value, axis, [(i, (i + by) % size) for i in range(size)])]
    broadcast_in_dim x3 -> x0, local copies, waits for them, and re-layouts: 3.4 us -> none  [the longest x1 2.69 us: body(): jnp.broadcast_to(q[None], (plane, blocks, 128, 128))]
    unnamed x32 -> x12, local copies, waits for them, and re-layouts: 2.83 us -> 0.04 us
    all_to_all x1, waiting for transfers between devices: 10.1 us -> 7.62 us  [body(): lax.all_to_all(grad_partial.reshape(ring, blocks, 128, 128), ('row', 'dep...]
  transfers between devices with their start and end apart: 16 -> 21, of which waited for: 8 -> 10; matrix products, arithmetic and copies ran while one was open for 2% -> 3% of each run, Pallas kernels for 3% -> 5%
where the time goes in v2:
time: 109 us; the launch traced here: 108 us
  starting transfers between devices  49.9 us (46%)
  waiting for transfers between devices  40.3 us (37%)
  Pallas kernels  12.4 us (11%)
  other arithmetic  3.36 us (3%)
  between operations  1.49 us (1%)
    ppermute x15, waiting for transfers between devices, shift(): lax.ppermute(value, axis, [(i, (i + by) % size) for i in range(size)])  28.6 us
    ppermute x15, starting transfers between devices, shift(): lax.ppermute(value, axis, [(i, (i + by) % size) for i in range(size)])  22.5 us
    all_to_all x1, starting transfers between devices, body(): lax.all_to_all(summed.reshape(chips, half, 128), plane, 0, 0, tiled=True)  10.5 us
    all_to_all x1, starting transfers between devices, body(): lax.all_to_all(grad_partial.reshape(ring, blocks, 128, 128), ('row', 'dep...  7.93 us
    all_to_all x1, waiting for transfers between devices, body(): lax.all_to_all(grad_partial.reshape(ring, blocks, 128, 128), ('row', 'dep...  7.62 us
    all_to_all x1, starting transfers between devices, body(): lax.all_to_all(q, plane, 0, 0, tiled=True).reshape(chips * blocks, 128, 128)  5.43 us
    pallas_call x1, Pallas kernels, body(): pl.pallas_call(forward_kernel, in_specs=[smem] * 3 + [hbm] * 5, out_specs...  4.88 us
    pallas_call x1, Pallas kernels, body(): pl.pallas_call(backward_kernel, in_specs=[smem] * 3 + [hbm] * 3, out_spec...  4.62 us
  transfers between devices with their start and end apart: 21, of which 10 were waited for; matrix products, arithmetic and copies ran while one was open for 3% of the time, Pallas kernels for 5%

profile of v2, /device:TPU:4, one launch (start us, length us, event | category | flops | bytes accessed | tf_op | source)
XLA Modules:
  0.0 108.1 jit_solution(7660889504206256165)
XLA Ops:
  0.6 3.3 %collective-permute-start = (bf16[512,128]{1,0:T(8,128)(2,1)}, bf16[512,128]{1,0:T(8,128)(2,1)S(1)}, u32[]{:S(2)}, u32[]{:S(2)}) collective-permute-start(bf16[512,128]{1,0:T(8,128)(2,1)} %x.3), channel_id=1, source_target_pairs={{0,64},{32,96},{64,0},{96,32},{1,65},{33,97},{65,1},{97,33},{2,66}... | collective-permute-start | bytes 393224 | tf_op jit(solution)/shard_map/ppermute | solution.py:180
  4.6 2.6 %collective-permute-start.2 = (bf16[512,128]{1,0:T(8,128)(2,1)}, bf16[512,128]{1,0:T(8,128)(2,1)S(1)}, u32[]{:S(2)}, u32[]{:S(2)}) collective-permute-start(bf16[512,128]{1,0:T(8,128)(2,1)} %x.3), channel_id=1, source_target_pairs={{0,96},{32,0},{64,32},{96,64},{1,97},{33,1},{65,33},{97,65},{2,98}... | collective-permute-start | bytes 393224 | tf_op jit(solution)/shard_map/ppermute | solution.py:180
  8.6 2.3 %collective-permute-done.1.x2 = bf16[512,128]{1,0:T(8,128)(2,1)S(1)} collective-permute-done((bf16[512,128]{1,0:T(8,128)(2,1)}, bf16[512,128]{1,0:T(8,128)(2,1)S(1)}, u32[]{:S(2)}, u32[]{:S(2)}) %collective-permute-start.1) | collective-permute-done | bytes 131104 | tf_op jit(solution)/shard_map/ppermute | solution.py:180
  10.8 4.9 %forward.1 = (f32[8192,128]{1,0:T(8,128)S(1)}, bf16[4096,128]{1,0:T(8,128)(2,1)S(1)}) custom-call(s32[1]{0:T(128)S(6)} %copy.14.live, s32[256]{0:T(256)S(1)} %get-tuple-element.39.into, s32[256]{0:T(256)S(1)} %get-tuple-element.40.source, bf16[512,128]{1,0:T(8,128)(2,1)} %x.3, bf16[512,128]{1,0:T(8,128)(2,1)S(1)} %collective-permute-done.x1, ...), custom_call_target="tpu_custom_call" | custom-call | tf_op jit(solution)/shard_map/forward/pallas_call | solution.py:248
  15.9 2.6 %collective-permute-done.3 = bf16[4096,128]{1,0:T(8,128)(2,1)S(1)} collective-permute-done((bf16[4096,128]{1,0:T(8,128)(2,1)S(1)}, bf16[4096,128]{1,0:T(8,128)(2,1)S(1)}, u32[]{:S(2)}, u32[]{:S(2)}) %collective-permute-start.3) | collective-permute-done | bytes 1048608 | tf_op jit(solution)/shard_map/ppermute | solution.py:180
  18.5 1.2 %add_convert_fusion = bf16[4096,128]{1,0:T(8,128)(2,1)} fusion(bf16[4096,128]{1,0:T(8,128)(2,1)S(1)} %collective-permute-done.3, f32[8192,128]{1,0:T(8,128)S(1)} %get-tuple-element.19), kind=kLoop, calls=%fused_computation | loop fusion | flops 1572864 | bytes 4194304 | tf_op jit(solution)/shard_map/convert_element_type | solution.py:262
  19.7 10.5 %all-to-all-start = ((bf16[16,256,128]{2,1,0:T(8,128)(2,1)}), bf16[16,256,128]{2,1,0:T(8,128)(2,1)S(1)}, u32[]{:S(2)}, u32[]{:S(2)}) async-start(bf16[16,256,128]{2,1,0:T(8,128)(2,1)} %bitcast.2), calls=%async_computation | async-start | bytes 2097152 | tf_op jit(solution)/shard_map/all_to_all | solution.py:263
  30.2 3.1 %collective-permute-start.4 = (bf16[528,128]{1,0:T(8,128)(2,1)S(1)}, bf16[528,128]{1,0:T(8,128)(2,1)S(1)}, u32[]{:S(2)}, u32[]{:S(2)}) collective-permute-start(bf16[528,128]{1,0:T(8,128)(2,1)S(1)} %pack.1), channel_id=1, source_target_pairs={{0,1},{1,0},{2,3},{3,2},{4,5},{5,4},{6,7},{7,6},{8,9},{9,8},{10,11... | collective-permute-start | bytes 405512 | tf_op jit(solution)/shard_map/ppermute | solution.py:180
  33.3 14.9 %collective-permute-done.4.packed = bf16[528,128]{1,0:T(8,128)(2,1)S(1)} collective-permute-done((bf16[528,128]{1,0:T(8,128)(2,1)S(1)}, bf16[528,128]{1,0:T(8,128)(2,1)S(1)}, u32[]{:S(2)}, u32[]{:S(2)}) %collective-permute-start.4) | collective-permute-done | bytes 135200 | tf_op jit(solution)/shard_map/ppermute | solution.py:180
  48.1 1.6 %shard_map.128 = (bf16[256,128]{1,0:T(8,128)(2,1)S(1)}, bf16[256,128]{1,0:T(8,128)(2,1)S(1)}, bf16[16,2,128,128]{3,2,1,0:T(8,128)(2,1)}, bf16[256,128]{1,0:T(8,1...) custom-call(bf16[16,256,128]{2,1,0:T(8,128)(2,1)S(1)} %all-to-all-done.parts,, ...), custom_call_target="tpu_custom_call" | custom-call | tf_op jit(solution)/shard_map/pallas_call | solution.py:267
  49.8 5.4 %all-to-all-start.1 = ((bf16[16,2,128,128]{3,2,1,0:T(8,128)(2,1)}), bf16[16,2,128,128]{3,2,1,0:T(8,128)(2,1)S(1)}, u32[]{:S(2)}, u32[]{:S(2)}) async-start(bf16[16,2,128,128]{3,2,1,0:T(8,128)(2,1)} %get-tuple-element.23), calls=%async_computation.1 | async-start | bytes 2097152 | tf_op jit(solution)/shard_map/all_to_all | solution.py:281
  55.8 1.3 %collective-permute-done.6 = f32[2,136,128]{2,1,0:T(8,128)S(1)} collective-permute-done((f32[2,136,128]{2,1,0:T(8,128)S(1)}, f32[2,136,128]{2,1,0:T(8,128)S(1)}, u32[]{:S(2)}, u32[]{:S(2)}) %collective-permute-start.6) | collective-permute-done | bytes 139296 | tf_op jit(solution)/shard_map/ppermute | solution.py:180
  57.8 4.8 %collective-permute-start.8 = (f32[2,136,128]{2,1,0:T(8,128)S(1)}, f32[2,136,128]{2,1,0:T(8,128)S(1)}, u32[]{:S(2)}, u32[]{:S(2)}) collective-permute-start(f32[2,136,128]{2,1,0:T(8,128)S(1)} %add.91), channel_id=1, source_target_pairs={{0,64},{32,96},{64,0},{96,32},{1,65},{33,97},{65,1},{97,33},{2,66}... | collective-permute-start | bytes 417800 | tf_op jit(solution)/shard_map/ppermute | solution.py:180
  62.6 2.5 %collective-permute-done.7 = f32[2,136,128]{2,1,0:T(8,128)S(1)} collective-permute-done((f32[2,136,128]{2,1,0:T(8,128)S(1)}, f32[2,136,128]{2,1,0:T(8,128)S(1)}, u32[]{:S(2)}, u32[]{:S(2)}) %collective-permute-start.7) | collective-permute-done | bytes 139296 | tf_op jit(solution)/shard_map/ppermute | solution.py:180
  65.1 4.2 %collective-permute-done.8 = f32[2,136,128]{2,1,0:T(8,128)S(1)} collective-permute-done((f32[2,136,128]{2,1,0:T(8,128)S(1)}, f32[2,136,128]{2,1,0:T(8,128)S(1)}, u32[]{:S(2)}, u32[]{:S(2)}) %collective-permute-start.8) | collective-permute-done | bytes 139296 | tf_op jit(solution)/shard_map/ppermute | solution.py:180
  69.4 3.1 %collective-permute-start.5 = (bf16[256,128]{1,0:T(8,128)(2,1)S(1)}, bf16[256,128]{1,0:T(8,128)(2,1)S(1)}, u32[]{:S(2)}, u32[]{:S(2)}) collective-permute-start(bf16[256,128]{1,0:T(8,128)(2,1)S(1)} %get-tuple-element.22), channel_id=1, source_target_pairs={{0,1},{1,0},{2,3},{3,2},{4,5},{5,4},{6,7},{7,6},{8,9},{9,8},{10,11... | collective-permute-start | bytes 196616 | tf_op jit(solution)/shard_map/ppermute | solution.py:180
  73.1 2.7 %collective-permute-start.13 = (f32[136,128]{1,0:T(8,128)S(1)}, f32[136,128]{1,0:T(8,128)S(1)}, u32[]{:S(2)}, u32[]{:S(2)}) collective-permute-start(f32[136,128]{1,0:T(8,128)S(1)} %get-tuple-element.34), channel_id=1, source_target_pairs={{0,5},{1,4},{4,1},{5,0},{2,7},{3,6},{6,3},{7,2},{8,13},{9,12},{12,... | collective-permute-start | bytes 208904 | tf_op jit(solution)/shard_map/ppermute | solution.py:296
  76.1 4.0 %collective-permute-done.11 = f32[136,128]{1,0:T(8,128)S(1)} collective-permute-done((f32[136,128]{1,0:T(8,128)S(1)}, f32[136,128]{1,0:T(8,128)S(1)}, u32[]{:S(2)}, u32[]{:S(2)}) %collective-permute-start.11) | collective-permute-done | bytes 69664 | tf_op jit(solution)/shard_map/ppermute | solution.py:296
  80.1 1.2 %collective-permute-start.14 = (f32[136,128]{1,0:T(8,128)S(1)}, f32[136,128]{1,0:T(8,128)S(1)}, u32[]{:S(2)}, u32[]{:S(2)}) collective-permute-start(f32[136,128]{1,0:T(8,128)S(1)} %add_add_fusion.1), channel_id=1, source_target_pairs={{0,8},{8,16},{16,24},{24,0},{1,9},{9,17},{17,25},{25,1},{2,10},{10... | collective-permute-start | bytes 208904 | tf_op jit(solution)/shard_map/ppermute | solution.py:180
  81.4 0.9 collective-permute-start.15
  82.2 2.2 %collective-permute-start.16 = (f32[136,128]{1,0:T(8,128)S(1)}, f32[136,128]{1,0:T(8,128)S(1)}, u32[]{:S(2)}, u32[]{:S(2)}) collective-permute-start(f32[136,128]{1,0:T(8,128)S(1)} %add_add_fusion.1), channel_id=1, source_target_pairs={{0,24},{8,0},{16,8},{24,16},{1,25},{9,1},{17,9},{25,17},{2,26},{10... | collective-permute-start | bytes 208904 | tf_op jit(solution)/shard_map/ppermute | solution.py:180
  85.1 4.6 %backward.1 = bf16[16,128,128]{2,1,0:T(8,128)(2,1)} custom-call(s32[1]{0:T(128)S(6)} %copy.14.live, s32[256]{0:T(256)S(1)} %get-tuple-element.39.into, s32[256]{0:T(256)S(1)} %bitcast.17, bf16[32,128,128]{2,1,0:T(8,128)(2,1)S(1)} %bitcast.15, bf16[32,128,128]{2,1,0:T(8,128)(2,1)S(1)} %collective-permute-done.10.q_other, bf16[256,128,128]{2,1,0:T(8,128)(2,1)} %tiles.3), custom_call_target="tpu_custom_call" | custom-call | tf_op jit(solution)/shard_map/backward/pallas_call | solution.py:306
  89.7 7.9 %all-to-all-start.2 = ((bf16[8,2,128,128]{3,2,1,0:T(8,128)(2,1)}), bf16[8,2,128,128]{3,2,1,0:T(8,128)(2,1)S(1)}, u32[]{:S(2)}, u32[]{:S(2)}) async-start(bf16[8,2,128,128]{3,2,1,0:T(8,128)(2,1)} %bitcast.5), calls=%async_computation.2 | async-start | bytes 1048576 | tf_op jit(solution)/shard_map/all_to_all | solution.py:323
  99.7 7.6 %all-to-all-done.2.parts = bf16[8,2,128,128]{3,2,1,0:T(8,128)(2,1)S(1)} async-done(((bf16[8,2,128,128]{3,2,1,0:T(8,128)(2,1)}), bf16[8,2,128,128]{3,2,1,0:T(8,128)(2,1)S(1)}, u32[]{:S(2)}, u32[]{:S(2)}) %all-to-all-start.2) | async-done | bytes 524320 | tf_op jit(solution)/shard_map/all_to_all | solution.py:323
  (48 shorter events, 7.3 us)
Async XLA Ops:
  0.6 7.9 %collective-permute-start = (bf16[512,128]{1,0:T(8,128)(2,1)}, bf16[512,128]{1,0:T(8,128)(2,1)S(1)}, u32[]{:S(2)}, u32[]{:S(2)}) collective-permute-start(bf16[512,128]{1,0:T(8,128)(2,1)} %x.3), channel_id=1, source_target_pairs={{0,64},{32,96},{64,0},{96,32},{1,65},{33,97},{65,1},{97,33},{2,66}... | collective-permute-start | bytes 393224 | tf_op jit(solution)/shard_map/ppermute | solution.py:180
  3.9 6.9 %collective-permute-start.1 = (bf16[512,128]{1,0:T(8,128)(2,1)}, bf16[512,128]{1,0:T(8,128)(2,1)S(1)}, u32[]{:S(2)}, u32[]{:S(2)}) collective-permute-start(bf16[512,128]{1,0:T(8,128)(2,1)} %x.3), channel_id=1, source_target_pairs={{0,32},{32,64},{64,96},{96,0},{1,33},{33,65},{65,97},{97,1},{2,34}... | collective-permute-start | bytes 393224 | tf_op jit(solution)/shard_map/ppermute | solution.py:180
  4.6 6.3 %collective-permute-start.2 = (bf16[512,128]{1,0:T(8,128)(2,1)}, bf16[512,128]{1,0:T(8,128)(2,1)S(1)}, u32[]{:S(2)}, u32[]{:S(2)}) collective-permute-start(bf16[512,128]{1,0:T(8,128)(2,1)} %x.3), channel_id=1, source_target_pairs={{0,96},{32,0},{64,32},{96,64},{1,97},{33,1},{65,33},{97,65},{2,98}... | collective-permute-start | bytes 393224 | tf_op jit(solution)/shard_map/ppermute | solution.py:180
  15.7 14.5 %copy-start.1 = (bf16[512,128]{1,0:T(8,128)(2,1)S(1)}, bf16[512,128]{1,0:T(8,128)(2,1)}, u32[]{:S(2)}) copy-start(bf16[512,128]{1,0:T(8,128)(2,1)} %cot_a.1) | copy-start | bytes 393220
  15.8 32.4 %copy-start = (bf16[512,128]{1,0:T(8,128)(2,1)S(1)}, bf16[512,128]{1,0:T(8,128)(2,1)}, u32[]{:S(2)}) copy-start(bf16[512,128]{1,0:T(8,128)(2,1)} %x.3) | copy-start | bytes 393220
  15.8 2.7 %collective-permute-start.3 = (bf16[4096,128]{1,0:T(8,128)(2,1)S(1)}, bf16[4096,128]{1,0:T(8,128)(2,1)S(1)}, u32[]{:S(2)}, u32[]{:S(2)}) collective-permute-start(bf16[4096,128]{1,0:T(8,128)(2,1)S(1)} %get-tuple-element.20), channel_id=1, source_target_pairs={{0,2},{2,0},{1,3},{3,1},{4,6},{6,4},{5,7},{7,5},{8,10},{10,8},{9,1... | collective-permute-start | bytes 3145736 | tf_op jit(solution)/shard_map/ppermute | solution.py:180
  19.7 65.4 %copy-start.4 = (s32[1,256]{1,0:T(1,128)S(1)}, s32[1,256]{1,0:T(1,128)}, u32[]{:S(2)}) copy-start(s32[1,256]{1,0:T(1,128)} %param.16) | copy-start | bytes 3076
  19.7 28.4 %all-to-all-start = ((bf16[16,256,128]{2,1,0:T(8,128)(2,1)}), bf16[16,256,128]{2,1,0:T(8,128)(2,1)S(1)}, u32[]{:S(2)}, u32[]{:S(2)}) async-start(bf16[16,256,128]{2,1,0:T(8,128)(2,1)} %bitcast.2), calls=%async_computation | async-start | bytes 2097152 | tf_op jit(solution)/shard_map/all_to_all | solution.py:263
  30.2 17.9 %collective-permute-start.4 = (bf16[528,128]{1,0:T(8,128)(2,1)S(1)}, bf16[528,128]{1,0:T(8,128)(2,1)S(1)}, u32[]{:S(2)}, u32[]{:S(2)}) collective-permute-start(bf16[528,128]{1,0:T(8,128)(2,1)S(1)} %pack.1), channel_id=1, source_target_pairs={{0,1},{1,0},{2,3},{3,2},{4,5},{5,4},{6,7},{7,6},{8,9},{9,8},{10,11... | collective-permute-start | bytes 405512 | tf_op jit(solution)/shard_map/ppermute | solution.py:180
  49.8 19.5 %all-to-all-start.1 = ((bf16[16,2,128,128]{3,2,1,0:T(8,128)(2,1)}), bf16[16,2,128,128]{3,2,1,0:T(8,128)(2,1)S(1)}, u32[]{:S(2)}, u32[]{:S(2)}) async-start(bf16[16,2,128,128]{3,2,1,0:T(8,128)(2,1)} %get-tuple-element.23), calls=%async_computation.1 | async-start | bytes 2097152 | tf_op jit(solution)/shard_map/all_to_all | solution.py:281
  55.7 1.4 %collective-permute-start.6 = (f32[2,136,128]{2,1,0:T(8,128)S(1)}, f32[2,136,128]{2,1,0:T(8,128)S(1)}, u32[]{:S(2)}, u32[]{:S(2)}) collective-permute-start(f32[2,136,128]{2,1,0:T(8,128)S(1)} %get-tuple-element.29), channel_id=1, source_target_pairs={{0,2},{2,0},{1,3},{3,1},{4,6},{6,4},{5,7},{7,5},{8,10},{10,8},{9,1... | collective-permute-start | bytes 417800 | tf_op jit(solution)/shard_map/ppermute | solution.py:180
  57.2 7.9 %collective-permute-start.7 = (f32[2,136,128]{2,1,0:T(8,128)S(1)}, f32[2,136,128]{2,1,0:T(8,128)S(1)}, u32[]{:S(2)}, u32[]{:S(2)}) collective-permute-start(f32[2,136,128]{2,1,0:T(8,128)S(1)} %add.91), channel_id=1, source_target_pairs={{0,32},{32,64},{64,96},{96,0},{1,33},{33,65},{65,97},{97,1},{2,34}... | collective-permute-start | bytes 417800 | tf_op jit(solution)/shard_map/ppermute | solution.py:180
  57.8 11.5 %collective-permute-start.8 = (f32[2,136,128]{2,1,0:T(8,128)S(1)}, f32[2,136,128]{2,1,0:T(8,128)S(1)}, u32[]{:S(2)}, u32[]{:S(2)}) collective-permute-start(f32[2,136,128]{2,1,0:T(8,128)S(1)} %add.91), channel_id=1, source_target_pairs={{0,64},{32,96},{64,0},{96,32},{1,65},{33,97},{65,1},{97,33},{2,66}... | collective-permute-start | bytes 417800 | tf_op jit(solution)/shard_map/ppermute | solution.py:180
  62.6 6.7 %collective-permute-start.9 = (f32[2,136,128]{2,1,0:T(8,128)S(1)}, f32[2,136,128]{2,1,0:T(8,128)S(1)}, u32[]{:S(2)}, u32[]{:S(2)}) collective-permute-start(f32[2,136,128]{2,1,0:T(8,128)S(1)} %add.91), channel_id=1, source_target_pairs={{0,96},{32,0},{64,32},{96,64},{1,97},{33,1},{65,33},{97,65},{2,98}... | collective-permute-start | bytes 417800 | tf_op jit(solution)/shard_map/ppermute | solution.py:180
  69.3 15.7 %collective-permute-start.10 = (bf16[32,128,128]{2,1,0:T(8,128)(2,1)S(1)}, bf16[32,128,128]{2,1,0:T(8,128)(2,1)S(1)}, u32[]{:S(2)}, u32[]{:S(2)}) collective-permute-start(bf16[32,128,128]{2,1,0:T(8,128)(2,1)S(1)} %bitcast.14), channel_id=1, source_target_pairs={{0,2},{2,0},{1,3},{3,1},{4,6},{6,4},{5,7},{7,5},{8,10},{10,8},{9,1... | collective-permute-start | bytes 3145736 | tf_op jit(solution)/shard_map/ppermute | solution.py:180
  69.4 6.6 %collective-permute-start.5 = (bf16[256,128]{1,0:T(8,128)(2,1)S(1)}, bf16[256,128]{1,0:T(8,128)(2,1)S(1)}, u32[]{:S(2)}, u32[]{:S(2)}) collective-permute-start(bf16[256,128]{1,0:T(8,128)(2,1)S(1)} %get-tuple-element.22), channel_id=1, source_target_pairs={{0,1},{1,0},{2,3},{3,2},{4,5},{5,4},{6,7},{7,6},{8,9},{9,8},{10,11... | collective-permute-start | bytes 196616 | tf_op jit(solution)/shard_map/ppermute | solution.py:180
  72.5 7.6 %collective-permute-start.12 = (f32[136,128]{1,0:T(8,128)S(1)}, f32[136,128]{1,0:T(8,128)S(1)}, u32[]{:S(2)}, u32[]{:S(2)}) collective-permute-start(f32[136,128]{1,0:T(8,128)S(1)} %get-tuple-element.34), channel_id=1, source_target_pairs={{0,1},{1,0},{4,5},{5,4},{2,3},{3,2},{6,7},{7,6},{8,9},{9,8},{12,13... | collective-permute-start | bytes 208904 | tf_op jit(solution)/shard_map/ppermute | solution.py:296
  73.1 7.0 %collective-permute-start.13 = (f32[136,128]{1,0:T(8,128)S(1)}, f32[136,128]{1,0:T(8,128)S(1)}, u32[]{:S(2)}, u32[]{:S(2)}) collective-permute-start(f32[136,128]{1,0:T(8,128)S(1)} %get-tuple-element.34), channel_id=1, source_target_pairs={{0,5},{1,4},{4,1},{5,0},{2,7},{3,6},{6,3},{7,2},{8,13},{9,12},{12,... | collective-permute-start | bytes 208904 | tf_op jit(solution)/shard_map/ppermute | solution.py:296
  75.8 4.3 %collective-permute-start.11 = (f32[136,128]{1,0:T(8,128)S(1)}, f32[136,128]{1,0:T(8,128)S(1)}, u32[]{:S(2)}, u32[]{:S(2)}) collective-permute-start(f32[136,128]{1,0:T(8,128)S(1)} %get-tuple-element.33), channel_id=1, source_target_pairs={{0,4},{1,5},{4,0},{5,1},{2,6},{3,7},{6,2},{7,3},{8,12},{9,13},{12,... | collective-permute-start | bytes 208904 | tf_op jit(solution)/shard_map/ppermute | solution.py:296
  80.1 17.5 %collective-permute-start.14 = (f32[136,128]{1,0:T(8,128)S(1)}, f32[136,128]{1,0:T(8,128)S(1)}, u32[]{:S(2)}, u32[]{:S(2)}) collective-permute-start(f32[136,128]{1,0:T(8,128)S(1)} %add_add_fusion.1), channel_id=1, source_target_pairs={{0,8},{8,16},{16,24},{24,0},{1,9},{9,17},{17,25},{25,1},{2,10},{10... | collective-permute-start | bytes 208904 | tf_op jit(solution)/shard_map/ppermute | solution.py:180
  81.4 16.3 %collective-permute-start.15 = (f32[136,128]{1,0:T(8,128)S(1)}, f32[136,128]{1,0:T(8,128)S(1)}, u32[]{:S(2)}, u32[]{:S(2)}) collective-permute-start(f32[136,128]{1,0:T(8,128)S(1)} %add_add_fusion.1), channel_id=1, source_target_pairs={{0,16},{8,24},{16,0},{24,8},{1,17},{9,25},{17,1},{25,9},{2,18},{10... | collective-permute-start | bytes 208904 | tf_op jit(solution)/shard_map/ppermute | solution.py:180
  82.2 15.4 %collective-permute-start.16 = (f32[136,128]{1,0:T(8,128)S(1)}, f32[136,128]{1,0:T(8,128)S(1)}, u32[]{:S(2)}, u32[]{:S(2)}) collective-permute-start(f32[136,128]{1,0:T(8,128)S(1)} %add_add_fusion.1), channel_id=1, source_target_pairs={{0,24},{8,0},{16,8},{24,16},{1,25},{9,1},{17,9},{25,17},{2,26},{10... | collective-permute-start | bytes 208904 | tf_op jit(solution)/shard_map/ppermute | solution.py:180
  89.7 17.6 %all-to-all-start.2 = ((bf16[8,2,128,128]{3,2,1,0:T(8,128)(2,1)}), bf16[8,2,128,128]{3,2,1,0:T(8,128)(2,1)S(1)}, u32[]{:S(2)}, u32[]{:S(2)}) async-start(bf16[8,2,128,128]{3,2,1,0:T(8,128)(2,1)} %bitcast.5), calls=%async_computation.2 | async-start | bytes 1048576 | tf_op jit(solution)/shard_map/all_to_all | solution.py:323
  97.7 1.3 %collective-permute-start.17 = (f32[128,128]{1,0:T(8,128)S(1)}, f32[128,128]{1,0:T(8,128)S(1)}, u32[]{:S(2)}, u32[]{:S(2)}) collective-permute-start(f32[128,128]{1,0:T(8,128)S(1)} %slice.22), channel_id=1, source_target_pairs={{0,2},{2,0},{1,3},{3,1},{4,6},{6,4},{5,7},{7,5},{8,10},{10,8},{9,1... | collective-permute-start | bytes 196616 | tf_op jit(solution)/shard_map/ppermute | solution.py:180
  (3 other events, 43.4 us)

commit v3 on v2

--- a/solution.py
+++ b/solution.py
@@ -7,6 +7,8 @@
 
 
 GROUP = 32
+AHEAD = 3
+HEAD = 3
 F32 = jnp.float32
 BF16 = jnp.bfloat16
 
@@ -23,34 +25,54 @@
     return lax.dot_general(a, b, (((0,), (0,)), ((), ())), preferred_element_type=F32)
 
 
-def tile_copy(group, tiles, tile_buf, sems):
-    at = pl.ds(group * GROUP, GROUP)
-    return pltpu.make_async_copy(tiles.at[at], tile_buf.at[at], sems.at[group])
-
-
-def start_tiles(live_groups, tiles, tile_buf, sems):
+def tile_copy(group, first, tiles, tile_buf, sems):
+    size = pl.ds(group * GROUP, GROUP)
+    at = pl.ds((group - first) * GROUP, GROUP)
+    return pltpu.make_async_copy(tiles.at[size], tile_buf.at[at], sems.at[group])
+
+
+def head_copies(live_groups, tiles, head, sems, act):
+    for group in range(HEAD):
+
+        @pl.when(group < live_groups)
+        def _(group=group):
+            copy = tile_copy(group, 0, tiles, head, sems)
+            copy.start() if act == "start" else copy.wait()
+
+
+def start_tail(live_groups, tiles, tail, sems):
     def start(group, carry):
-        tile_copy(group, tiles, tile_buf, sems).start()
+        tile_copy(group, HEAD, tiles, tail, sems).start()
         return carry
 
-    lax.fori_loop(0, live_groups, start, 0)
-
-
-def for_tiles(live_groups, tiles, tile_buf, sems, step):
-    def one_group(group, carry):
-        tile_copy(group, tiles, tile_buf, sems).wait()
+    lax.fori_loop(HEAD, jnp.minimum(live_groups, HEAD + AHEAD), start, 0)
+
+
+def for_tiles(live_groups, tiles, head, tail, sems, step):
+    def head_group(group, carry):
         for k in range(GROUP):
-            step(group * GROUP + k)
+            step(head[group * GROUP + k], group * GROUP + k)
         return carry
 
-    lax.fori_loop(0, live_groups, one_group, 0)
+    def tail_group(group, carry):
+        tile_copy(group, HEAD, tiles, tail, sems).wait()
+
+        @pl.when(group + AHEAD < live_groups)
+        def _():
+            tile_copy(group + AHEAD, HEAD, tiles, tail, sems).start()
+
+        for k in range(GROUP):
+            step(tail[(group - HEAD) * GROUP + k], group * GROUP + k)
+        return carry
+
+    lax.fori_loop(0, jnp.minimum(live_groups, HEAD), head_group, 0)
+    lax.fori_loop(HEAD, live_groups, tail_group, 0)
 
 
 def forward_kernel(
-    live, into, source, x0, x1, x2, x3, tiles, acc, other, x_buf, tile_buf, sems, x_sems
+    live, into, source, x0, x1, x2, x3, tiles, head, zeros, acc, other, x_buf, tail, sems, x_sems
 ):
     live_groups = live[0] // GROUP
-    start_tiles(live_groups, tiles, tile_buf, sems)
     span = x0.shape[0]
     copies = [
         pltpu.make_async_copy(shard, x_buf.at[pl.ds(k * span, span)], x_sems.at[k])
@@ -58,46 +80,57 @@
     ]
     for copy in copies:
         copy.start()
-    acc[...] = jnp.zeros_like(acc)
+    start_tail(live_groups, tiles, tail, sems)
     for copy in copies:
         copy.wait()
 
-    def step(t):
-        block = x_buf[pl.ds(pl.multiple_of(source[t] * 128, 128), 128), :]
-        target = pl.ds(pl.multiple_of(into[t] * 128, 128), 128)
-        acc[target, :] += dot_nn(tile_buf[t], block)
-
-    for_tiles(live_groups, tiles, tile_buf, sems, step)
-    other[...] = acc[other.shape[0] :, :].astype(BF16)
-
-
-def backward_kernel(live, into, cols, q_own, q_other, tiles, out, q_buf, tile_buf, acc, sems, q_sems):
+    def step(tile, t):
+        acc[into[t]] += dot_nn(tile, x_buf[source[t]])
+
+    for_tiles(live_groups, tiles, head, tail, sems, step)
+    other[...] = acc[other.shape[0] :].astype(BF16)
+
+
+def ready_kernel(live, q_own, tiles, head, q_buf, sems, q_sem):
     live_groups = live[0] // GROUP
-    start_tiles(live_groups, tiles, tile_buf, sems)
-    half = q_own.shape[0]
+    copy = pltpu.make_async_copy(q_own, q_buf.at[pl.ds(0, q_own.shape[0])], q_sem)
+    copy.start()
+    head_copies(live_groups, tiles, head, sems, "start")
+    copy.wait()
+    head_copies(live_groups, tiles, head, sems, "wait")
+
+
+def backward_kernel(
+    live, into, cols, q_other, tiles, head, q_half, out, q_buf, tail, acc, sems, q_sem
+):
+    live_groups = live[0] // GROUP
+    half = q_other.shape[0]
+    copy = pltpu.make_async_copy(q_other, q_buf.at[pl.ds(half, half)], q_sem)
+    copy.start()
+    start_tail(live_groups, tiles, tail, sems)
+    acc[...] = jnp.zeros_like(acc)
+    copy.wait()
+
+    def step(tile, t):
+        acc[cols[t]] += dot_nn(q_buf[into[t]], tile)
+
+    for_tiles(live_groups, tiles, head, tail, sems, step)
+    out[...] = acc[...].astype(BF16)
+
+
+def prepare_kernel(live, bias, cot, ws, wn, tiles, packed, head, acc, sems, tile_sems):
+    live_groups = live[0] // GROUP
+    half = cot.shape[0] // 2
+    other = 1 - lax.axis_index("depth")
     copies = [
-        pltpu.make_async_copy(part, q_buf.at[pl.ds(k * half, half)], q_sems.at[k])
-        for k, part in enumerate((q_own, q_other))
+        pltpu.make_async_copy(part, packed.at[pl.ds(at, part.shape[0])], sems.at[k])
+        for k, (part, at) in enumerate(
+            ((cot.at[pl.ds(other * half, half)], 0), (ws, half), (wn, half + 128))
+        )
     ]
     for copy in copies:
         copy.start()
-    acc[...] = jnp.zeros_like(acc)
-    for copy in copies:
-        copy.wait()
-
-    def step(t):
-        acc[cols[t]] += dot_nn(q_buf[into[t]], tile_buf[t])
-
-    for_tiles(live_groups, tiles, tile_buf, sems, step)
-    out[...] = acc[...].astype(BF16)
-
-
-def pack_kernel(cot, ws, wn, bias, packed):
-    half = cot.shape[0] // 2
-    other = 1 - lax.axis_index("depth")
-    packed[0:half] = cot[pl.ds(other * half, half), :]
-    packed[half : half + 128] = ws[...]
-    packed[half + 128 : half + 256] = wn[...]
+    head_copies(live_groups, tiles, head, tile_sems, "start")
     first = bias[...].astype(BF16)
     rest = bias[...] - first.astype(F32)
     second = rest.astype(BF16)
@@ -105,6 +138,10 @@
     row = lax.broadcasted_iota(jnp.int32, (16, 128), 0)
     lines = jnp.where(row == 0, first.astype(F32), jnp.where(row == 1, second.astype(F32), third.astype(F32)))
     packed[half + 256 : half + 272] = jnp.where(row < 3, lines, 0.0).astype(BF16)
+    acc[...] = jnp.zeros_like(acc)
+    for copy in copies:
+        copy.wait()
+    head_copies(live_groups, tiles, head, tile_sems, "wait")
 
 
 def own_part(ref):
@@ -204,32 +241,46 @@
     own_row = lax.axis_index("row")
     own_core = lax.axis_index("core")
     own_depth = lax.axis_index("depth")
-    plane = ("depth", "near", "x")
+    plane = ("near", "depth", "x")
     chips = lax.axis_size("x") * lax.axis_size("near") * lax.axis_size("depth")
     vmem = pl.BlockSpec(memory_space=pltpu.VMEM)
     smem = pl.BlockSpec(memory_space=pltpu.SMEM)
     hbm = pl.BlockSpec(memory_space=pl.ANY)
-    scratch_tiles = pltpu.VMEM((slots, 128, 128), BF16)
     tile_sems = pltpu.SemaphoreType.DMA((slots // GROUP,))
 
     def in_vmem(value):
         return pltpu.with_memory_space_constraint(value, pltpu.VMEM)
 
-    shards = [pltpu.with_memory_space_constraint(features, pltpu.HBM)] + [
-        in_vmem(shift(features, "row", k)) for k in (2, 1, 3)
-    ]
+    moved = [features] + [shift(features, "row", k) for k in (2, 1, 3)]
+    moved = [value.reshape(span // 128, 128, 128) for value in moved]
+    shards = [pltpu.with_memory_space_constraint(moved[0], pltpu.HBM)]
+    shards += [in_vmem(value) for value in moved[1:]]
     own_bias = bias[None, :]
-    packed = pl.pallas_call(
-        pack_kernel,
-        in_specs=[vmem] * 4,
-        out_specs=vmem,
-        out_shape=pltpu.VMEM((half + 272, 128), BF16),
-        compiler_params=pltpu.CompilerParams(vmem_limit_bytes=4 * 1024 * 1024),
-        name="pack",
-    )(cotangent, self_weight, neigh_weight, own_bias)
+
+    def in_hbm(value):
+        return pltpu.with_memory_space_constraint(value, pltpu.HBM)
+
+    tiles = in_hbm(tile_values)
+    head_shape = pltpu.VMEM((HEAD * GROUP, 128, 128), BF16)
+    tail_scratch = pltpu.VMEM((slots - HEAD * GROUP, 128, 128), BF16)
+    packed, head, zeros = pl.pallas_call(
+        prepare_kernel,
+        in_specs=[smem, vmem] + [hbm] * 4,
+        out_specs=[vmem] * 3,
+        out_shape=[
+            pltpu.VMEM((half + 272, 128), BF16),
+            head_shape,
+            pltpu.VMEM((2 * chips * blocks, 128, 128), F32),
+        ],
+        scratch_shapes=[pltpu.SemaphoreType.DMA((3,)), tile_sems],
+        compiler_params=pltpu.CompilerParams(vmem_limit_bytes=2 * 1024 * 1024),
+        name="prepare",
+    )(
+        tile_counts, in_hbm(own_bias), in_hbm(cotangent), in_hbm(self_weight),
+        in_hbm(neigh_weight), tiles,
+    )
     packed = shift(packed, "depth", 1)
 
-    tiles = pltpu.with_memory_space_constraint(tile_values, pltpu.HBM)
     rows = tile_rows[0]
     cols = tile_cols[0]
     span_blocks = span // 128
@@ -237,29 +288,36 @@
     source = jnp.where(behind == 1, 2, jnp.where(behind == 2, 1, behind)) * span_blocks
     source = source + cols % span_blocks
     owner = rows // blocks
-    chip = owner % 2 * 8 + owner // 4 % 2 * 4 + owner // 8
+    part = {"depth": owner % 2, "near": owner // 4 % 2, "x": owner // 8}
+    chip = 0
+    for axis in plane:
+        chip = chip * lax.axis_size(axis) + part[axis]
     apart = (owner // 2 % 2) ^ own_core
     into = (apart * chips + chip) * blocks + rows % blocks
-    half_rows = chips * half
 
     def build_shape(shape, dtype):
         return jax.ShapeDtypeStruct(shape, dtype)
 
     acc, other = pl.pallas_call(
         forward_kernel,
-        in_specs=[smem] * 3 + [hbm] * 5,
+        in_specs=[smem] * 3 + [hbm] * 5 + [vmem] * 2,
+        input_output_aliases={9: 0},
         out_specs=[vmem, vmem],
-        out_shape=[pltpu.VMEM((2 * half_rows, 128), F32), pltpu.VMEM((half_rows, 128), BF16)],
+        out_shape=[
+            pltpu.VMEM((2 * chips * blocks, 128, 128), F32),
+            pltpu.VMEM((chips * blocks, 128, 128), BF16),
+        ],
         scratch_shapes=[
-            pltpu.VMEM((span * row_count, 128), BF16),
-            scratch_tiles,
+            pltpu.VMEM((span * row_count // 128, 128, 128), BF16),
+            tail_scratch,
             tile_sems,
             pltpu.SemaphoreType.DMA((row_count,)),
         ],
         compiler_params=pltpu.CompilerParams(vmem_limit_bytes=16 * 1024 * 1024),
         name="forward",
-    )(tile_counts, into, source, *shards, tiles)
-    summed = (acc[:half_rows] + shift(other, "core", 1).astype(F32)).astype(BF16)
+    )(tile_counts, into, source, *shards, tiles, in_vmem(head), in_vmem(zeros))
+    other = shift(other, "core", 1)
+    summed = (acc[: chips * blocks] + other.astype(F32)).astype(BF16)
     parts = lax.all_to_all(summed.reshape(chips, half, 128), plane, 0, 0, tiled=True)
     parts = in_vmem(parts)
 
@@ -288,7 +346,8 @@
     )
     out_received = shift(out_other, "depth", 1)
     gw = keep + shift(send, "core", 1)
-    gw = sum_over(gw, "row")
+    sent = gw.astype(BF16)
+    gw = gw + sum(shift(sent, "row", k).astype(F32) for k in range(1, row_count))
     q_own, gw = lax.optimization_barrier((q_own, gw))
     q_other = in_vmem(shift(q_own, "core", 1))
     near = lax.axis_size("near")
@@ -303,21 +362,31 @@
     gw = gw[0] + moves[0] + moves[1] + moves[2]
     gw = sum_over(gw, "x")
     col_blocks = span * row_count // 128
-    grad_partial = pl.pallas_call(
+    q_shape = pltpu.VMEM((2 * chips * blocks, 128, 128), BF16)
+    head, q_buf = pl.pallas_call(
+        ready_kernel,
+        in_specs=[smem, vmem, hbm],
+        out_specs=[vmem] * 2,
+        out_shape=[head_shape, q_shape],
+        scratch_shapes=[tile_sems, pltpu.SemaphoreType.DMA],
+        compiler_params=pltpu.CompilerParams(vmem_limit_bytes=2 * 1024 * 1024),
+        name="ready",
+    )(tile_counts, q_own, tiles)
+    grad_partial, _ = pl.pallas_call(
         backward_kernel,
-        in_specs=[smem] * 3 + [hbm] * 3,
-        out_specs=vmem,
-        out_shape=pltpu.VMEM((col_blocks, 128, 128), BF16),
+        in_specs=[smem] * 3 + [vmem, hbm, vmem, vmem],
+        input_output_aliases={6: 1},
+        out_specs=[vmem] * 2,
+        out_shape=[pltpu.VMEM((col_blocks, 128, 128), BF16), q_shape],
         scratch_shapes=[
-            pltpu.VMEM((2 * chips * blocks, 128, 128), BF16),
-            scratch_tiles,
+            tail_scratch,
             pltpu.VMEM((col_blocks, 128, 128), F32),
             tile_sems,
-            pltpu.SemaphoreType.DMA((2,)),
+            pltpu.SemaphoreType.DMA,
         ],
         compiler_params=pltpu.CompilerParams(vmem_limit_bytes=16 * 1024 * 1024),
         name="backward",
-    )(tile_counts, into, cols, q_own, q_other, tiles)
+    )(tile_counts, into, cols, q_other, tiles, in_vmem(head), in_vmem(q_buf))
     ring = row_count * 2
     grad_parts = in_vmem(
         lax.all_to_all(

time: 109 us -> 108 us (level)
  starting transfers between devices: 49.9 us -> 41 us
  waiting for transfers between devices: 40.3 us -> 46.9 us
  Pallas kernels: 12.4 us -> 14.8 us
    ppermute x15, starting transfers between devices: 22.5 us -> 16.5 us  [shift(): lax.ppermute(value, axis, [(i, (i + by) % size) for i in range(size)])]
    all_to_all x1, waiting for transfers between devices: 0.06 us -> 5.12 us  [body(): lax.all_to_all(q, plane, 0, 0, tiled=True).reshape(chips * blocks, 128, 128)]
    pallas_call x3 -> x4, Pallas kernels: 9.52 us -> 11.9 us  [the longest x1 3.61 us: body(): pl.pallas_call(forward_kernel, in_specs=[smem] * 3 + [hbm] * 5 + [vmem] *...]
    all_to_all x1, starting transfers between devices: 7.93 us -> 5.69 us  [body(): lax.all_to_all(grad_partial.reshape(ring, blocks, 128, 128), ('row', 'dep...]
    ppermute x15, waiting for transfers between devices: 28.6 us -> 30.6 us  [shift(): lax.ppermute(value, axis, [(i, (i + by) % size) for i in range(size)])]
    all_to_all x1, starting transfers between devices: 10.5 us -> 9.06 us  [body(): lax.all_to_all(summed.reshape(chips, half, 128), plane, 0, 0, tiled=True)]
  transfers between devices with their start and end apart: 21 -> 21, of which waited for: 10 -> 13; matrix products, arithmetic and copies ran while one was open for 3% -> 2% of each run, Pallas kernels for 5% -> 8%
where the time goes in v3:
time: 108 us
  waiting for transfers between devices  46.9 us (43%)
  starting transfers between devices  41 us (38%)
  Pallas kernels  14.8 us (14%)
  other arithmetic  2.77 us (3%)
  between operations  1.5 us (1%)
    ppermute x15, waiting for transfers between devices, shift(): lax.ppermute(value, axis, [(i, (i + by) % size) for i in range(size)])  30.6 us
    ppermute x15, starting transfers between devices, shift(): lax.ppermute(value, axis, [(i, (i + by) % size) for i in range(size)])  16.5 us
    all_to_all x1, starting transfers between devices, body(): lax.all_to_all(summed.reshape(chips, half, 128), plane, 0, 0, tiled=True)  9.06 us
    all_to_all x1, waiting for transfers between devices, body(): lax.all_to_all(grad_partial.reshape(ring, blocks, 128, 128), ('row', 'dep...  7.62 us
    all_to_all x1, starting transfers between devices, body(): lax.all_to_all(grad_partial.reshape(ring, blocks, 128, 128), ('row', 'dep...  5.69 us
    all_to_all x1, starting transfers between devices, body(): lax.all_to_all(q, plane, 0, 0, tiled=True).reshape(chips * blocks, 128, 128)  5.58 us
    all_to_all x1, waiting for transfers between devices, body(): lax.all_to_all(q, plane, 0, 0, tiled=True).reshape(chips * blocks, 128, 128)  5.12 us
    ppermute x3, starting transfers between devices, body(): lax.ppermute(gw[flip], ('near', 'depth'), [(n * 2 + d, (n ^ step) * 2 + (...  4.17 us
  transfers between devices with their start and end apart: 21, of which 13 were waited for; matrix products, arithmetic and copies ran while one was open for 2% of the time, Pallas kernels for 8%

profile of v3, /device:TPU:4, one launch (start us, length us, event | category | flops | bytes accessed | tf_op | source)
XLA Modules:
  0.0 107.5 jit_solution(3678345746286851058)
XLA Ops:
  0.6 3.1 %collective-permute-start.2 = (bf16[512,128]{1,0:T(8,128)(2,1)}, bf16[512,128]{1,0:T(8,128)(2,1)S(1)}, u32[]{:S(2)}, u32[]{:S(2)}) collective-permute-start(bf16[512,128]{1,0:T(8,128)(2,1)} %x.3), channel_id=1, source_target_pairs={{0,96},{32,0},{64,32},{96,64},{1,97},{33,1},{65,33},{97,65},{2,98}... | collective-permute-start | bytes 393224 | tf_op jit(solution)/shard_map/ppermute | solution.py:217
  3.7 2.2 %collective-permute-start = (bf16[512,128]{1,0:T(8,128)(2,1)}, bf16[512,128]{1,0:T(8,128)(2,1)S(1)}, u32[]{:S(2)}, u32[]{:S(2)}) collective-permute-start(bf16[512,128]{1,0:T(8,128)(2,1)} %x.3), channel_id=1, source_target_pairs={{0,64},{32,96},{64,0},{96,32},{1,65},{33,97},{65,1},{97,33},{2,66}... | collective-permute-start | bytes 393224 | tf_op jit(solution)/shard_map/ppermute | solution.py:217
  6.6 2.7 %prepare.1 = (bf16[528,128]{1,0:T(8,128)(2,1)S(1)}, bf16[96,128,128]{2,1,0:T(8,128)(2,1)S(1)}, f32[64,128,128]{2,1,0:T(8,128)S(1)}) custom-call(s32[1]{0:T(128)S(6)} %copy.18.live, f32[1,128]{1,0:T(1,128)} %bitcast.26, bf16[512,128]{1,0:T(8,128)(2,1)} %cot_a.1, bf16[128,128]{1,0:T(8,128)(2,1)} %ws_a.3, bf16[128,128]{1,0:T(8,128)(2,1)} %wn_a.1, ...), custom_call_target="tpu_custom_call" | custom-call | tf_op jit(solution)/shard_map/prepare/pallas_call | solution.py:266
  9.4 3.5 %collective-permute-done.1 = bf16[512,128]{1,0:T(8,128)(2,1)S(1)} collective-permute-done((bf16[512,128]{1,0:T(8,128)(2,1)}, bf16[512,128]{1,0:T(8,128)(2,1)S(1)}, u32[]{:S(2)}, u32[]{:S(2)}) %collective-permute-start.1) | collective-permute-done | bytes 131104 | tf_op jit(solution)/shard_map/ppermute | solution.py:217
  12.9 3.6 %forward.1 = (f32[64,128,128]{2,1,0:T(8,128)S(1)}, bf16[32,128,128]{2,1,0:T(8,128)(2,1)S(1)}) custom-call(s32[1]{0:T(128)S(6)} %copy.18.live, s32[256]{0:T(256)S(1)} %get-tuple-element.53.into, s32[256]{0:T(256)S(1)} %get-tuple-element.54.source, bf16[4,128,128]{2,1,0:T(8,128)(2,1)} %bitcast.20, ...), custom_call_target="tpu_custom_call", output_to_operand_aliasing={{0}: (9, {})} | custom-call | tf_op jit(solution)/shard_map/forward/pallas_call | solution.py:301
  16.6 2.6 %collective-permute-done.3 = bf16[32,128,128]{2,1,0:T(8,128)(2,1)S(1)} collective-permute-done((bf16[32,128,128]{2,1,0:T(8,128)(2,1)S(1)}, bf16[32,128,128]{2,1,0:T(8,128)(2,1)S(1)}, u32[]{:S(2)}, u32[]{:S(2)}) %collective-permute-start.3) | collective-permute-done | bytes 1048608 | tf_op jit(solution)/shard_map/ppermute | solution.py:217
  19.3 1.3 %add_convert_fusion = bf16[32,128,128]{2,1,0:T(8,128)(2,1)} fusion(bf16[32,128,128]{2,1,0:T(8,128)(2,1)S(1)} %collective-permute-done.3, f32[64,128,128]{2,1,0:T(8,128)S(1)} %get-tuple-element.27), kind=kLoop, calls=%fused_computation | loop fusion | flops 1572864 | bytes 4194304 | tf_op jit(solution)/shard_map/convert_element_type | solution.py:320
  20.6 9.1 %all-to-all-start = ((bf16[16,256,128]{2,1,0:T(8,128)(2,1)}), bf16[16,256,128]{2,1,0:T(8,128)(2,1)S(1)}, u32[]{:S(2)}, u32[]{:S(2)}) async-start(bf16[16,256,128]{2,1,0:T(8,128)(2,1)} %bitcast.7), calls=%async_computation | async-start | bytes 2097152 | tf_op jit(solution)/shard_map/all_to_all | solution.py:321
  29.6 3.0 %collective-permute-start.4 = (bf16[528,128]{1,0:T(8,128)(2,1)S(1)}, bf16[528,128]{1,0:T(8,128)(2,1)S(1)}, u32[]{:S(2)}, u32[]{:S(2)}) collective-permute-start(bf16[528,128]{1,0:T(8,128)(2,1)S(1)} %get-tuple-element.29), channel_id=1, source_target_pairs={{0,1},{1,0},{2,3},{3,2},{4,5},{5,4},{6,7},{7,6},{8,9},{9,8},{10,11... | collective-permute-start | bytes 405512 | tf_op jit(solution)/shard_map/ppermute | solution.py:217
  32.6 15.2 %collective-permute-done.4.packed = bf16[528,128]{1,0:T(8,128)(2,1)S(1)} collective-permute-done((bf16[528,128]{1,0:T(8,128)(2,1)S(1)}, bf16[528,128]{1,0:T(8,128)(2,1)S(1)}, u32[]{:S(2)}, u32[]{:S(2)}) %collective-permute-start.4) | collective-permute-done | bytes 135200 | tf_op jit(solution)/shard_map/ppermute | solution.py:217
  47.8 1.7 %shard_map.128 = (bf16[256,128]{1,0:T(8,128)(2,1)S(1)}, bf16[256,128]{1,0:T(8,128)(2,1)S(1)}, bf16[16,2,128,128]{3,2,1,0:T(8,128)(2,1)}, bf16[256,128]{1,0:T(8,1...) custom-call(bf16[16,256,128]{2,1,0:T(8,128)(2,1)S(1)} %all-to-all-done.parts,, ...), custom_call_target="tpu_custom_call" | custom-call | tf_op jit(solution)/shard_map/pallas_call | solution.py:325
  49.5 5.6 %all-to-all-start.1 = ((bf16[16,2,128,128]{3,2,1,0:T(8,128)(2,1)}), bf16[16,2,128,128]{3,2,1,0:T(8,128)(2,1)S(1)}, u32[]{:S(2)}, u32[]{:S(2)}) async-start(bf16[16,2,128,128]{3,2,1,0:T(8,128)(2,1)} %get-tuple-element.32), calls=%async_computation.1 | async-start | bytes 2097152 | tf_op jit(solution)/shard_map/all_to_all | solution.py:339
  55.7 1.3 %collective-permute-done.6 = f32[2,136,128]{2,1,0:T(8,128)S(1)} collective-permute-done((f32[2,136,128]{2,1,0:T(8,128)S(1)}, f32[2,136,128]{2,1,0:T(8,128)S(1)}, u32[]{:S(2)}, u32[]{:S(2)}) %collective-permute-start.6) | collective-permute-done | bytes 139296 | tf_op jit(solution)/shard_map/ppermute | solution.py:217
  59.2 2.9 %collective-permute-done.9 = bf16[2,136,128]{2,1,0:T(8,128)(2,1)S(1)} collective-permute-done((bf16[2,136,128]{2,1,0:T(8,128)(2,1)S(1)}, bf16[2,136,128]{2,1,0:T(8,128)(2,1)S(1)}, u32[]{:S(2)}, u32[]{:S(2)}) %collective-permute-start.9) | collective-permute-done | bytes 69664 | tf_op jit(solution)/shard_map/ppermute | solution.py:217
  62.1 2.6 %collective-permute-done.8 = bf16[2,136,128]{2,1,0:T(8,128)(2,1)S(1)} collective-permute-done((bf16[2,136,128]{2,1,0:T(8,128)(2,1)S(1)}, bf16[2,136,128]{2,1,0:T(8,128)(2,1)S(1)}, u32[]{:S(2)}, u32[]{:S(2)}) %collective-permute-start.8) | collective-permute-done | bytes 69664 | tf_op jit(solution)/shard_map/ppermute | solution.py:217
  65.2 5.1 %all-to-all-done.1 = bf16[16,2,128,128]{3,2,1,0:T(8,128)(2,1)S(1)} async-done(((bf16[16,2,128,128]{3,2,1,0:T(8,128)(2,1)}), bf16[16,2,128,128]{3,2,1,0:T(8,128)(2,1)S(1)}, u32[]{:S(2)}, u32[]{:S(2)}) %all-to-all-start.1) | async-done | bytes 1048608 | tf_op jit(solution)/shard_map/all_to_all | solution.py:339
  71.1 2.6 %collective-permute-start.13 = (f32[136,128]{1,0:T(8,128)S(1)}, f32[136,128]{1,0:T(8,128)S(1)}, u32[]{:S(2)}, u32[]{:S(2)}) collective-permute-start(f32[136,128]{1,0:T(8,128)S(1)} %get-tuple-element.48), channel_id=1, source_target_pairs={{0,5},{1,4},{4,1},{5,0},{2,7},{3,6},{6,3},{7,2},{8,13},{9,12},{12,... | collective-permute-start | bytes 208904 | tf_op jit(solution)/shard_map/ppermute | solution.py:355
  76.5 2.4 %collective-permute-done.11 = f32[136,128]{1,0:T(8,128)S(1)} collective-permute-done((f32[136,128]{1,0:T(8,128)S(1)}, f32[136,128]{1,0:T(8,128)S(1)}, u32[]{:S(2)}, u32[]{:S(2)}) %collective-permute-start.11) | collective-permute-done | bytes 69664 | tf_op jit(solution)/shard_map/ppermute | solution.py:355
  81.1 2.1 %collective-permute-start.15 = (f32[136,128]{1,0:T(8,128)S(1)}, f32[136,128]{1,0:T(8,128)S(1)}, u32[]{:S(2)}, u32[]{:S(2)}) collective-permute-start(f32[136,128]{1,0:T(8,128)S(1)} %add_add_fusion.1), channel_id=1, source_target_pairs={{0,16},{8,24},{16,0},{24,8},{1,17},{9,25},{17,1},{25,9},{2,18},{10... | collective-permute-start | bytes 208904 | tf_op jit(solution)/shard_map/ppermute | solution.py:217
  83.2 1.9 %collective-permute-start.14 = (f32[136,128]{1,0:T(8,128)S(1)}, f32[136,128]{1,0:T(8,128)S(1)}, u32[]{:S(2)}, u32[]{:S(2)}) collective-permute-start(f32[136,128]{1,0:T(8,128)S(1)} %add_add_fusion.1), channel_id=1, source_target_pairs={{0,8},{8,16},{16,24},{24,0},{1,9},{9,17},{17,25},{25,1},{2,10},{10... | collective-permute-start | bytes 208904 | tf_op jit(solution)/shard_map/ppermute | solution.py:217
  85.8 2.0 %ready.1 = (bf16[96,128,128]{2,1,0:T(8,128)(2,1)S(1)}, bf16[64,128,128]{2,1,0:T(8,128)(2,1)S(1)}) custom-call(s32[1]{0:T(128)S(6)} %copy.18.live, bf16[32,128,128]{2,1,0:T(8,128)(2,1)S(1)} %bitcast.19, bf16[256,128,128]{2,1,0:T(8,128)(2,1)} %tiles.7), custom_call_target="tpu_custom_call" | custom-call | tf_op jit(solution)/shard_map/ready/pallas_call | solution.py:366
  87.8 3.6 %backward.1 = (bf16[16,128,128]{2,1,0:T(8,128)(2,1)}, bf16[64,128,128]{2,1,0:T(8,128)(2,1)S(1)}) custom-call(s32[1]{0:T(128)S(6)} %copy.18.live, s32[256]{0:T(256)S(1)} %get-tuple-element.53.into, s32[256]{0:T(256)S(1)} %bitcast.25, bf16[32,128,128]{2,1,0:T(8,128)(2,1)S(1)} %collective-permute-done.10.q_other, ...), custom_call_target="tpu_custom_call", output_to_operand_aliasing={{1}: (6, {})} | custom-call | tf_op jit(solution)/shard_map/backward/pallas_call | solution.py:375
  91.4 5.7 %all-to-all-start.2 = ((bf16[8,2,128,128]{3,2,1,0:T(8,128)(2,1)}), bf16[8,2,128,128]{3,2,1,0:T(8,128)(2,1)S(1)}, u32[]{:S(2)}, u32[]{:S(2)}) async-start(bf16[8,2,128,128]{3,2,1,0:T(8,128)(2,1)} %bitcast.9), calls=%async_computation.2 | async-start | bytes 1048576 | tf_op jit(solution)/shard_map/all_to_all | solution.py:392
  99.1 7.6 %all-to-all-done.2.parts = bf16[8,2,128,128]{3,2,1,0:T(8,128)(2,1)S(1)} async-done(((bf16[8,2,128,128]{3,2,1,0:T(8,128)(2,1)}), bf16[8,2,128,128]{3,2,1,0:T(8,128)(2,1)S(1)}, u32[]{:S(2)}, u32[]{:S(2)}) %all-to-all-start.2) | async-done | bytes 524320 | tf_op jit(solution)/shard_map/all_to_all | solution.py:392
  (51 shorter events, 12.7 us)
Async XLA Ops:
  0.6 8.7 %collective-permute-start.2 = (bf16[512,128]{1,0:T(8,128)(2,1)}, bf16[512,128]{1,0:T(8,128)(2,1)S(1)}, u32[]{:S(2)}, u32[]{:S(2)}) collective-permute-start(bf16[512,128]{1,0:T(8,128)(2,1)} %x.3), channel_id=1, source_target_pairs={{0,96},{32,0},{64,32},{96,64},{1,97},{33,1},{65,33},{97,65},{2,98}... | collective-permute-start | bytes 393224 | tf_op jit(solution)/shard_map/ppermute | solution.py:217
  3.7 9.2 %collective-permute-start.1 = (bf16[512,128]{1,0:T(8,128)(2,1)}, bf16[512,128]{1,0:T(8,128)(2,1)S(1)}, u32[]{:S(2)}, u32[]{:S(2)}) collective-permute-start(bf16[512,128]{1,0:T(8,128)(2,1)} %x.3), channel_id=1, source_target_pairs={{0,32},{32,64},{64,96},{96,0},{1,33},{33,65},{65,97},{97,1},{2,34}... | collective-permute-start | bytes 393224 | tf_op jit(solution)/shard_map/ppermute | solution.py:217
  3.7 9.2 %collective-permute-start = (bf16[512,128]{1,0:T(8,128)(2,1)}, bf16[512,128]{1,0:T(8,128)(2,1)S(1)}, u32[]{:S(2)}, u32[]{:S(2)}) collective-permute-start(bf16[512,128]{1,0:T(8,128)(2,1)} %x.3), channel_id=1, source_target_pairs={{0,64},{32,96},{64,0},{96,32},{1,65},{33,97},{65,1},{97,33},{2,66}... | collective-permute-start | bytes 393224 | tf_op jit(solution)/shard_map/ppermute | solution.py:217
  16.5 2.7 %collective-permute-start.3 = (bf16[32,128,128]{2,1,0:T(8,128)(2,1)S(1)}, bf16[32,128,128]{2,1,0:T(8,128)(2,1)S(1)}, u32[]{:S(2)}, u32[]{:S(2)}) collective-permute-start(bf16[32,128,128]{2,1,0:T(8,128)(2,1)S(1)} %get-tuple-element.28), channel_id=1, source_target_pairs={{0,2},{2,0},{1,3},{3,1},{4,6},{6,4},{5,7},{7,5},{8,10},{10,8},{9,1... | collective-permute-start | bytes 3145736 | tf_op jit(solution)/shard_map/ppermute | solution.py:217
  19.3 28.5 %copy-start.2 = (bf16[128,128]{1,0:T(8,128)(2,1)S(1)}, bf16[128,128]{1,0:T(8,128)(2,1)}, u32[]{:S(2)}) copy-start(bf16[128,128]{1,0:T(8,128)(2,1)} %ws_a.3) | copy-start | bytes 98308
  19.3 28.5 %copy-start.3 = (bf16[128,128]{1,0:T(8,128)(2,1)S(1)}, bf16[128,128]{1,0:T(8,128)(2,1)}, u32[]{:S(2)}) copy-start(bf16[128,128]{1,0:T(8,128)(2,1)} %wn_a.1) | copy-start | bytes 98308
  19.3 28.6 %copy-start.5 = (f32[128]{0:T(128)S(1)}, f32[128]{0:T(128)}, u32[]{:S(2)}) copy-start(f32[128]{0:T(128)} %param.12) | copy-start | bytes 1540
  20.6 27.2 %all-to-all-start = ((bf16[16,256,128]{2,1,0:T(8,128)(2,1)}), bf16[16,256,128]{2,1,0:T(8,128)(2,1)S(1)}, u32[]{:S(2)}, u32[]{:S(2)}) async-start(bf16[16,256,128]{2,1,0:T(8,128)(2,1)} %bitcast.7), calls=%async_computation | async-start | bytes 2097152 | tf_op jit(solution)/shard_map/all_to_all | solution.py:321
  29.6 18.2 %collective-permute-start.4 = (bf16[528,128]{1,0:T(8,128)(2,1)S(1)}, bf16[528,128]{1,0:T(8,128)(2,1)S(1)}, u32[]{:S(2)}, u32[]{:S(2)}) collective-permute-start(bf16[528,128]{1,0:T(8,128)(2,1)S(1)} %get-tuple-element.29), channel_id=1, source_target_pairs={{0,1},{1,0},{2,3},{3,2},{4,5},{5,4},{6,7},{7,6},{8,9},{9,8},{10,11... | collective-permute-start | bytes 405512 | tf_op jit(solution)/shard_map/ppermute | solution.py:217
  49.5 20.9 %all-to-all-start.1 = ((bf16[16,2,128,128]{3,2,1,0:T(8,128)(2,1)}), bf16[16,2,128,128]{3,2,1,0:T(8,128)(2,1)S(1)}, u32[]{:S(2)}, u32[]{:S(2)}) async-start(bf16[16,2,128,128]{3,2,1,0:T(8,128)(2,1)} %get-tuple-element.32), calls=%async_computation.1 | async-start | bytes 2097152 | tf_op jit(solution)/shard_map/all_to_all | solution.py:339
  55.6 1.4 %collective-permute-start.6 = (f32[2,136,128]{2,1,0:T(8,128)S(1)}, f32[2,136,128]{2,1,0:T(8,128)S(1)}, u32[]{:S(2)}, u32[]{:S(2)}) collective-permute-start(f32[2,136,128]{2,1,0:T(8,128)S(1)} %get-tuple-element.38), channel_id=1, source_target_pairs={{0,2},{2,0},{1,3},{3,1},{4,6},{6,4},{5,7},{7,5},{8,10},{10,8},{9,1... | collective-permute-start | bytes 417800 | tf_op jit(solution)/shard_map/ppermute | solution.py:217
  57.0 5.0 %collective-permute-start.9 = (bf16[2,136,128]{2,1,0:T(8,128)(2,1)S(1)}, bf16[2,136,128]{2,1,0:T(8,128)(2,1)S(1)}, u32[]{:S(2)}, u32[]{:S(2)}) collective-permute-start(bf16[2,136,128]{2,1,0:T(8,128)(2,1)S(1)} %get-tuple-element.45), channel_id=1, source_target_pairs={{0,96},{32,0},{64,32},{96,64},{1,97},{33,1},{65,33},{97,65},{2,98}... | collective-permute-start | bytes 208904 | tf_op jit(solution)/shard_map/ppermute | solution.py:217
  58.2 6.4 %collective-permute-start.8 = (bf16[2,136,128]{2,1,0:T(8,128)(2,1)S(1)}, bf16[2,136,128]{2,1,0:T(8,128)(2,1)S(1)}, u32[]{:S(2)}, u32[]{:S(2)}) collective-permute-start(bf16[2,136,128]{2,1,0:T(8,128)(2,1)S(1)} %get-tuple-element.45), channel_id=1, source_target_pairs={{0,64},{32,96},{64,0},{96,32},{1,65},{33,97},{65,1},{97,33},{2,66}... | collective-permute-start | bytes 208904 | tf_op jit(solution)/shard_map/ppermute | solution.py:217
  58.2 6.9 %collective-permute-start.7 = (bf16[2,136,128]{2,1,0:T(8,128)(2,1)S(1)}, bf16[2,136,128]{2,1,0:T(8,128)(2,1)S(1)}, u32[]{:S(2)}, u32[]{:S(2)}) collective-permute-start(bf16[2,136,128]{2,1,0:T(8,128)(2,1)S(1)} %get-tuple-element.45), channel_id=1, source_target_pairs={{0,32},{32,64},{64,96},{96,0},{1,33},{33,65},{65,97},{97,1},{2,34}... | collective-permute-start | bytes 208904 | tf_op jit(solution)/shard_map/ppermute | solution.py:217
  70.3 17.5 %collective-permute-start.10 = (bf16[32,128,128]{2,1,0:T(8,128)(2,1)S(1)}, bf16[32,128,128]{2,1,0:T(8,128)(2,1)S(1)}, u32[]{:S(2)}, u32[]{:S(2)}) collective-permute-start(bf16[32,128,128]{2,1,0:T(8,128)(2,1)S(1)} %bitcast.18), channel_id=1, source_target_pairs={{0,2},{2,0},{1,3},{3,1},{4,6},{6,4},{5,7},{7,5},{8,10},{10,8},{9,1... | collective-permute-start | bytes 3145736 | tf_op jit(solution)/shard_map/ppermute | solution.py:217
  70.4 6.1 %collective-permute-start.5 = (bf16[256,128]{1,0:T(8,128)(2,1)S(1)}, bf16[256,128]{1,0:T(8,128)(2,1)S(1)}, u32[]{:S(2)}, u32[]{:S(2)}) collective-permute-start(bf16[256,128]{1,0:T(8,128)(2,1)S(1)} %get-tuple-element.31), channel_id=1, source_target_pairs={{0,1},{1,0},{2,3},{3,2},{4,5},{5,4},{6,7},{7,6},{8,9},{9,8},{10,11... | collective-permute-start | bytes 196616 | tf_op jit(solution)/shard_map/ppermute | solution.py:217
  71.1 7.8 %collective-permute-start.13 = (f32[136,128]{1,0:T(8,128)S(1)}, f32[136,128]{1,0:T(8,128)S(1)}, u32[]{:S(2)}, u32[]{:S(2)}) collective-permute-start(f32[136,128]{1,0:T(8,128)S(1)} %get-tuple-element.48), channel_id=1, source_target_pairs={{0,5},{1,4},{4,1},{5,0},{2,7},{3,6},{6,3},{7,2},{8,13},{9,12},{12,... | collective-permute-start | bytes 208904 | tf_op jit(solution)/shard_map/ppermute | solution.py:355
  73.7 6.3 %collective-permute-start.12 = (f32[136,128]{1,0:T(8,128)S(1)}, f32[136,128]{1,0:T(8,128)S(1)}, u32[]{:S(2)}, u32[]{:S(2)}) collective-permute-start(f32[136,128]{1,0:T(8,128)S(1)} %get-tuple-element.48), channel_id=1, source_target_pairs={{0,1},{1,0},{4,5},{5,4},{2,3},{3,2},{6,7},{7,6},{8,9},{9,8},{12,13... | collective-permute-start | bytes 208904 | tf_op jit(solution)/shard_map/ppermute | solution.py:355
  74.1 4.8 %collective-permute-start.11 = (f32[136,128]{1,0:T(8,128)S(1)}, f32[136,128]{1,0:T(8,128)S(1)}, u32[]{:S(2)}, u32[]{:S(2)}) collective-permute-start(f32[136,128]{1,0:T(8,128)S(1)} %get-tuple-element.47), channel_id=1, source_target_pairs={{0,4},{1,5},{4,0},{5,1},{2,6},{3,7},{6,2},{7,3},{8,12},{9,13},{12,... | collective-permute-start | bytes 208904 | tf_op jit(solution)/shard_map/ppermute | solution.py:355
  80.0 17.1 %collective-permute-start.16 = (f32[136,128]{1,0:T(8,128)S(1)}, f32[136,128]{1,0:T(8,128)S(1)}, u32[]{:S(2)}, u32[]{:S(2)}) collective-permute-start(f32[136,128]{1,0:T(8,128)S(1)} %add_add_fusion.1), channel_id=1, source_target_pairs={{0,24},{8,0},{16,8},{24,16},{1,25},{9,1},{17,9},{25,17},{2,26},{10... | collective-permute-start | bytes 208904 | tf_op jit(solution)/shard_map/ppermute | solution.py:217
  81.1 15.9 %collective-permute-start.15 = (f32[136,128]{1,0:T(8,128)S(1)}, f32[136,128]{1,0:T(8,128)S(1)}, u32[]{:S(2)}, u32[]{:S(2)}) collective-permute-start(f32[136,128]{1,0:T(8,128)S(1)} %add_add_fusion.1), channel_id=1, source_target_pairs={{0,16},{8,24},{16,0},{24,8},{1,17},{9,25},{17,1},{25,9},{2,18},{10... | collective-permute-start | bytes 208904 | tf_op jit(solution)/shard_map/ppermute | solution.py:217
  83.2 13.9 %collective-permute-start.14 = (f32[136,128]{1,0:T(8,128)S(1)}, f32[136,128]{1,0:T(8,128)S(1)}, u32[]{:S(2)}, u32[]{:S(2)}) collective-permute-start(f32[136,128]{1,0:T(8,128)S(1)} %add_add_fusion.1), channel_id=1, source_target_pairs={{0,8},{8,16},{16,24},{24,0},{1,9},{9,17},{17,25},{25,1},{2,10},{10... | collective-permute-start | bytes 208904 | tf_op jit(solution)/shard_map/ppermute | solution.py:217
  91.4 15.4 %all-to-all-start.2 = ((bf16[8,2,128,128]{3,2,1,0:T(8,128)(2,1)}), bf16[8,2,128,128]{3,2,1,0:T(8,128)(2,1)S(1)}, u32[]{:S(2)}, u32[]{:S(2)}) async-start(bf16[8,2,128,128]{3,2,1,0:T(8,128)(2,1)} %bitcast.9), calls=%async_computation.2 | async-start | bytes 1048576 | tf_op jit(solution)/shard_map/all_to_all | solution.py:392
  97.1 1.3 %collective-permute-start.17 = (f32[128,128]{1,0:T(8,128)S(1)}, f32[128,128]{1,0:T(8,128)S(1)}, u32[]{:S(2)}, u32[]{:S(2)}) collective-permute-start(f32[128,128]{1,0:T(8,128)S(1)} %slice.22), channel_id=1, source_target_pairs={{0,2},{2,0},{1,3},{3,1},{4,6},{6,4},{5,7},{7,5},{8,10},{10,8},{9,1... | collective-permute-start | bytes 196616 | tf_op jit(solution)/shard_map/ppermute | solution.py:217
  (4 other events, 62.6 us)

commit v4 on v3

--- a/solution.py
+++ b/solution.py
@@ -348,18 +348,11 @@
     gw = keep + shift(send, "core", 1)
     sent = gw.astype(BF16)
     gw = gw + sum(shift(sent, "row", k).astype(F32) for k in range(1, row_count))
+    gw = gw + shift(gw.astype(BF16), "near", 1).astype(F32)
     q_own, gw = lax.optimization_barrier((q_own, gw))
     q_other = in_vmem(shift(q_own, "core", 1))
-    near = lax.axis_size("near")
-    moves = [
-        lax.ppermute(
-            gw[flip],
-            ("near", "depth"),
-            [(n * 2 + d, (n ^ step) * 2 + (d ^ flip)) for n in range(near) for d in range(2)],
-        )
-        for step, flip in ((1, 0), (0, 1), (1, 1))
-    ]
-    gw = gw[0] + moves[0] + moves[1] + moves[2]
+    moved_gw = shift(gw[1], "depth", 1)
+    gw = gw[0] + moved_gw
     gw = sum_over(gw, "x")
     col_blocks = span * row_count // 128
     q_shape = pltpu.VMEM((2 * chips * blocks, 128, 128), BF16)

time: 108 us -> 109 us (level)
    ppermute x15 -> x17, waiting for transfers between devices: 30.6 us -> 37.9 us  [shift(): lax.ppermute(value, axis, [(i, (i + by) % size) for i in range(size)])]
    ppermute x3 -> x0, starting transfers between devices: 4.17 us -> none  [body(): lax.ppermute(gw[flip], ('near', 'depth'), [(n * 2 + d, (n ^ step) * 2 + (...]
    all_to_all x1, waiting for transfers between devices: 5.12 us -> 1.35 us  [body(): lax.all_to_all(q, plane, 0, 0, tiled=True).reshape(chips * blocks, 128, 128)]
    ppermute x15 -> x17, starting transfers between devices: 16.5 us -> 20 us  [shift(): lax.ppermute(value, axis, [(i, (i + by) % size) for i in range(size)])]
    ppermute x3 -> x0, waiting for transfers between devices: 3.48 us -> none  [body(): lax.ppermute(gw[flip], ('near', 'depth'), [(n * 2 + d, (n ^ step) * 2 + (...]
    all_to_all x1, starting transfers between devices: 5.69 us -> 7 us  [body(): lax.all_to_all(grad_partial.reshape(ring, blocks, 128, 128), ('row', 'dep...]
  transfers between devices with their start and end apart: 21 -> 20, of which waited for: 13 -> 12; matrix products, arithmetic and copies ran while one was open for 2% -> 2% of each run, Pallas kernels for 8% -> 8%
where the time goes in v4:
time: 109 us; the launch traced here: 108 us
  waiting for transfers between devices  46.9 us (43%)
  starting transfers between devices  41.7 us (38%)
  Pallas kernels  14.8 us (14%)
  other arithmetic  2.8 us (3%)
  between operations  1.51 us (1%)
    ppermute x17, waiting for transfers between devices, shift(): lax.ppermute(value, axis, [(i, (i + by) % size) for i in range(size)])  37.9 us
    ppermute x17, starting transfers between devices, shift(): lax.ppermute(value, axis, [(i, (i + by) % size) for i in range(size)])  20 us
    all_to_all x1, starting transfers between devices, body(): lax.all_to_all(summed.reshape(chips, half, 128), plane, 0, 0, tiled=True)  9.06 us
    all_to_all x1, waiting for transfers between devices, body(): lax.all_to_all(grad_partial.reshape(ring, blocks, 128, 128), ('row', 'dep...  7.62 us
    all_to_all x1, starting transfers between devices, body(): lax.all_to_all(grad_partial.reshape(ring, blocks, 128, 128), ('row', 'dep...  7 us
    all_to_all x1, starting transfers between devices, body(): lax.all_to_all(q, plane, 0, 0, tiled=True).reshape(chips * blocks, 128, 128)  5.59 us
    pallas_call x1, Pallas kernels, body(): pl.pallas_call(forward_kernel, in_specs=[smem] * 3 + [hbm] * 5 + [vmem] *...  3.61 us
    pallas_call x1, Pallas kernels, body(): pl.pallas_call(backward_kernel, in_specs=[smem] * 3 + [vmem, hbm, vmem, v...  3.58 us
  transfers between devices with their start and end apart: 20, of which 12 were waited for; matrix products, arithmetic and copies ran while one was open for 2% of the time, Pallas kernels for 8%

profile of v4, /device:TPU:4, one launch (start us, length us, event | category | flops | bytes accessed | tf_op | source)
XLA Modules:
  0.0 108.3 jit_solution(4760109608774961162)
XLA Ops:
  0.6 3.1 %collective-permute-start.2 = (bf16[512,128]{1,0:T(8,128)(2,1)}, bf16[512,128]{1,0:T(8,128)(2,1)S(1)}, u32[]{:S(2)}, u32[]{:S(2)}) collective-permute-start(bf16[512,128]{1,0:T(8,128)(2,1)} %x.3), channel_id=1, source_target_pairs={{0,96},{32,0},{64,32},{96,64},{1,97},{33,1},{65,33},{97,65},{2,98}... | collective-permute-start | bytes 393224 | tf_op jit(solution)/shard_map/ppermute | solution.py:217
  3.7 2.2 %collective-permute-start = (bf16[512,128]{1,0:T(8,128)(2,1)}, bf16[512,128]{1,0:T(8,128)(2,1)S(1)}, u32[]{:S(2)}, u32[]{:S(2)}) collective-permute-start(bf16[512,128]{1,0:T(8,128)(2,1)} %x.3), channel_id=1, source_target_pairs={{0,64},{32,96},{64,0},{96,32},{1,65},{33,97},{65,1},{97,33},{2,66}... | collective-permute-start | bytes 393224 | tf_op jit(solution)/shard_map/ppermute | solution.py:217
  6.6 2.7 %prepare.1 = (bf16[528,128]{1,0:T(8,128)(2,1)S(1)}, bf16[96,128,128]{2,1,0:T(8,128)(2,1)S(1)}, f32[64,128,128]{2,1,0:T(8,128)S(1)}) custom-call(s32[1]{0:T(128)S(6)} %copy.18.live, f32[1,128]{1,0:T(1,128)} %bitcast.24, bf16[512,128]{1,0:T(8,128)(2,1)} %cot_a.1, bf16[128,128]{1,0:T(8,128)(2,1)} %ws_a.3, bf16[128,128]{1,0:T(8,128)(2,1)} %wn_a.1, ...), custom_call_target="tpu_custom_call" | custom-call | tf_op jit(solution)/shard_map/prepare/pallas_call | solution.py:266
  9.4 3.5 %collective-permute-done.1 = bf16[512,128]{1,0:T(8,128)(2,1)S(1)} collective-permute-done((bf16[512,128]{1,0:T(8,128)(2,1)}, bf16[512,128]{1,0:T(8,128)(2,1)S(1)}, u32[]{:S(2)}, u32[]{:S(2)}) %collective-permute-start.1) | collective-permute-done | bytes 131104 | tf_op jit(solution)/shard_map/ppermute | solution.py:217
  12.9 3.6 %forward.1 = (f32[64,128,128]{2,1,0:T(8,128)S(1)}, bf16[32,128,128]{2,1,0:T(8,128)(2,1)S(1)}) custom-call(s32[1]{0:T(128)S(6)} %copy.18.live, s32[256]{0:T(256)S(1)} %get-tuple-element.51.into, s32[256]{0:T(256)S(1)} %get-tuple-element.52.source, bf16[4,128,128]{2,1,0:T(8,128)(2,1)} %bitcast.18, ...), custom_call_target="tpu_custom_call", output_to_operand_aliasing={{0}: (9, {})} | custom-call | tf_op jit(solution)/shard_map/forward/pallas_call | solution.py:301
  16.6 2.6 %collective-permute-done.3 = bf16[32,128,128]{2,1,0:T(8,128)(2,1)S(1)} collective-permute-done((bf16[32,128,128]{2,1,0:T(8,128)(2,1)S(1)}, bf16[32,128,128]{2,1,0:T(8,128)(2,1)S(1)}, u32[]{:S(2)}, u32[]{:S(2)}) %collective-permute-start.3) | collective-permute-done | bytes 1048608 | tf_op jit(solution)/shard_map/ppermute | solution.py:217
  20.6 9.1 %all-to-all-start = ((bf16[16,256,128]{2,1,0:T(8,128)(2,1)}), bf16[16,256,128]{2,1,0:T(8,128)(2,1)S(1)}, u32[]{:S(2)}, u32[]{:S(2)}) async-start(bf16[16,256,128]{2,1,0:T(8,128)(2,1)} %bitcast.7), calls=%async_computation | async-start | bytes 2097152 | tf_op jit(solution)/shard_map/all_to_all | solution.py:321
  29.6 3.0 %collective-permute-start.4 = (bf16[528,128]{1,0:T(8,128)(2,1)S(1)}, bf16[528,128]{1,0:T(8,128)(2,1)S(1)}, u32[]{:S(2)}, u32[]{:S(2)}) collective-permute-start(bf16[528,128]{1,0:T(8,128)(2,1)S(1)} %get-tuple-element.29), channel_id=1, source_target_pairs={{0,1},{1,0},{2,3},{3,2},{4,5},{5,4},{6,7},{7,6},{8,9},{9,8},{10,11... | collective-permute-start | bytes 405512 | tf_op jit(solution)/shard_map/ppermute | solution.py:217
  32.6 15.2 %collective-permute-done.4.packed = bf16[528,128]{1,0:T(8,128)(2,1)S(1)} collective-permute-done((bf16[528,128]{1,0:T(8,128)(2,1)S(1)}, bf16[528,128]{1,0:T(8,128)(2,1)S(1)}, u32[]{:S(2)}, u32[]{:S(2)}) %collective-permute-start.4) | collective-permute-done | bytes 135200 | tf_op jit(solution)/shard_map/ppermute | solution.py:217
  47.8 1.7 %shard_map.128 = (bf16[256,128]{1,0:T(8,128)(2,1)S(1)}, bf16[256,128]{1,0:T(8,128)(2,1)S(1)}, bf16[16,2,128,128]{3,2,1,0:T(8,128)(2,1)}, bf16[256,128]{1,0:T(8,1...) custom-call(bf16[16,256,128]{2,1,0:T(8,128)(2,1)S(1)} %all-to-all-done.parts,, ...), custom_call_target="tpu_custom_call" | custom-call | tf_op jit(solution)/shard_map/pallas_call | solution.py:325
  50.1 5.6 %all-to-all-start.1 = ((bf16[16,2,128,128]{3,2,1,0:T(8,128)(2,1)}), bf16[16,2,128,128]{3,2,1,0:T(8,128)(2,1)S(1)}, u32[]{:S(2)}, u32[]{:S(2)}) async-start(bf16[16,2,128,128]{3,2,1,0:T(8,128)(2,1)} %get-tuple-element.32), calls=%async_computation.1 | async-start | bytes 2097152 | tf_op jit(solution)/shard_map/all_to_all | solution.py:339
  57.9 2.7 %collective-permute-done.9 = bf16[2,136,128]{2,1,0:T(8,128)(2,1)S(1)} collective-permute-done((bf16[2,136,128]{2,1,0:T(8,128)(2,1)S(1)}, bf16[2,136,128]{2,1,0:T(8,128)(2,1)S(1)}, u32[]{:S(2)}, u32[]{:S(2)}) %collective-permute-start.9) | collective-permute-done | bytes 69664 | tf_op jit(solution)/shard_map/ppermute | solution.py:217
  60.5 2.8 %collective-permute-done.8 = bf16[2,136,128]{2,1,0:T(8,128)(2,1)S(1)} collective-permute-done((bf16[2,136,128]{2,1,0:T(8,128)(2,1)S(1)}, bf16[2,136,128]{2,1,0:T(8,128)(2,1)S(1)}, u32[]{:S(2)}, u32[]{:S(2)}) %collective-permute-start.8) | collective-permute-done | bytes 69664 | tf_op jit(solution)/shard_map/ppermute | solution.py:217
  63.7 1.5 %collective-permute-start.10 = (bf16[2,136,128]{2,1,0:T(8,128)(2,1)S(1)}, bf16[2,136,128]{2,1,0:T(8,128)(2,1)S(1)}, u32[]{:S(2)}, u32[]{:S(2)}) collective-permute-start(bf16[2,136,128]{2,1,0:T(8,128)(2,1)S(1)} %fusion), channel_id=1, source_target_pairs={{0,4},{4,0},{1,5},{5,1},{2,6},{6,2},{3,7},{7,3},{8,12},{12,8},{9,1... | collective-permute-start | bytes 208904 | tf_op jit(solution)/shard_map/ppermute | solution.py:217
  65.3 5.6 %collective-permute-done.10 = bf16[2,136,128]{2,1,0:T(8,128)(2,1)S(1)} collective-permute-done((bf16[2,136,128]{2,1,0:T(8,128)(2,1)S(1)}, bf16[2,136,128]{2,1,0:T(8,128)(2,1)S(1)}, u32[]{:S(2)}, u32[]{:S(2)}) %collective-permute-start.10) | collective-permute-done | bytes 69664 | tf_op jit(solution)/shard_map/ppermute | solution.py:217
  72.2 2.2 %collective-permute-start.5 = (bf16[256,128]{1,0:T(8,128)(2,1)S(1)}, bf16[256,128]{1,0:T(8,128)(2,1)S(1)}, u32[]{:S(2)}, u32[]{:S(2)}) collective-permute-start(bf16[256,128]{1,0:T(8,128)(2,1)S(1)} %get-tuple-element.31), channel_id=1, source_target_pairs={{0,1},{1,0},{2,3},{3,2},{4,5},{5,4},{6,7},{7,6},{8,9},{9,8},{10,11... | collective-permute-start | bytes 196616 | tf_op jit(solution)/shard_map/ppermute | solution.py:217
  74.4 1.4 %collective-permute-start.12 = (f32[136,128]{1,0:T(8,128)S(1)}, f32[136,128]{1,0:T(8,128)S(1)}, u32[]{:S(2)}, u32[]{:S(2)}) collective-permute-start(f32[136,128]{1,0:T(8,128)S(1)} %slice_bitcast_fusion), channel_id=1, source_target_pairs={{0,1},{1,0},{2,3},{3,2},{4,5},{5,4},{6,7},{7,6},{8,9},{9,8},{10,11... | collective-permute-start | bytes 208904 | tf_op jit(solution)/shard_map/ppermute | solution.py:217
  75.8 2.5 %collective-permute-done.5 = bf16[256,128]{1,0:T(8,128)(2,1)S(1)} collective-permute-done((bf16[256,128]{1,0:T(8,128)(2,1)S(1)}, bf16[256,128]{1,0:T(8,128)(2,1)S(1)}, u32[]{:S(2)}, u32[]{:S(2)}) %collective-permute-start.5) | collective-permute-done | bytes 65568 | tf_op jit(solution)/shard_map/ppermute | solution.py:217
  78.3 2.0 %collective-permute-done.12 = f32[136,128]{1,0:T(8,128)S(1)} collective-permute-done((f32[136,128]{1,0:T(8,128)S(1)}, f32[136,128]{1,0:T(8,128)S(1)}, u32[]{:S(2)}, u32[]{:S(2)}) %collective-permute-start.12) | collective-permute-done | bytes 69664 | tf_op jit(solution)/shard_map/ppermute | solution.py:217
  80.7 3.0 %collective-permute-start.14 = (f32[136,128]{1,0:T(8,128)S(1)}, f32[136,128]{1,0:T(8,128)S(1)}, u32[]{:S(2)}, u32[]{:S(2)}) collective-permute-start(f32[136,128]{1,0:T(8,128)S(1)} %bitcast_add_fusion), channel_id=1, source_target_pairs={{0,16},{8,24},{16,0},{24,8},{1,17},{9,25},{17,1},{25,9},{2,18},{10... | collective-permute-start | bytes 208904 | tf_op jit(solution)/shard_map/ppermute | solution.py:217
  85.2 2.0 %ready.1 = (bf16[96,128,128]{2,1,0:T(8,128)(2,1)S(1)}, bf16[64,128,128]{2,1,0:T(8,128)(2,1)S(1)}) custom-call(s32[1]{0:T(128)S(6)} %copy.18.live, bf16[32,128,128]{2,1,0:T(8,128)(2,1)S(1)} %bitcast.17, bf16[256,128,128]{2,1,0:T(8,128)(2,1)} %tiles.7), custom_call_target="tpu_custom_call" | custom-call | tf_op jit(solution)/shard_map/ready/pallas_call | solution.py:359
  87.2 3.6 %backward.1 = (bf16[16,128,128]{2,1,0:T(8,128)(2,1)}, bf16[64,128,128]{2,1,0:T(8,128)(2,1)S(1)}) custom-call(s32[1]{0:T(128)S(6)} %copy.18.live, s32[256]{0:T(256)S(1)} %get-tuple-element.51.into, s32[256]{0:T(256)S(1)} %bitcast.23, bf16[32,128,128]{2,1,0:T(8,128)(2,1)S(1)} %collective-permute-done.11.q_other, ...), custom_call_target="tpu_custom_call", output_to_operand_aliasing={{1}: (6, {})} | custom-call | tf_op jit(solution)/shard_map/backward/pallas_call | solution.py:368
  90.8 7.0 %all-to-all-start.2 = ((bf16[8,2,128,128]{3,2,1,0:T(8,128)(2,1)}), bf16[8,2,128,128]{3,2,1,0:T(8,128)(2,1)S(1)}, u32[]{:S(2)}, u32[]{:S(2)}) async-start(bf16[8,2,128,128]{3,2,1,0:T(8,128)(2,1)} %bitcast.9), calls=%async_computation.2 | async-start | bytes 1048576 | tf_op jit(solution)/shard_map/all_to_all | solution.py:385
  99.9 7.6 %all-to-all-done.2.parts = bf16[8,2,128,128]{3,2,1,0:T(8,128)(2,1)S(1)} async-done(((bf16[8,2,128,128]{3,2,1,0:T(8,128)(2,1)}), bf16[8,2,128,128]{3,2,1,0:T(8,128)(2,1)S(1)}, u32[]{:S(2)}, u32[]{:S(2)}) %all-to-all-start.2) | async-done | bytes 524320 | tf_op jit(solution)/shard_map/all_to_all | solution.py:385
  (50 shorter events, 10.7 us)
Async XLA Ops:
  0.6 8.7 %collective-permute-start.2 = (bf16[512,128]{1,0:T(8,128)(2,1)}, bf16[512,128]{1,0:T(8,128)(2,1)S(1)}, u32[]{:S(2)}, u32[]{:S(2)}) collective-permute-start(bf16[512,128]{1,0:T(8,128)(2,1)} %x.3), channel_id=1, source_target_pairs={{0,96},{32,0},{64,32},{96,64},{1,97},{33,1},{65,33},{97,65},{2,98}... | collective-permute-start | bytes 393224 | tf_op jit(solution)/shard_map/ppermute | solution.py:217
  3.7 9.2 %collective-permute-start.1 = (bf16[512,128]{1,0:T(8,128)(2,1)}, bf16[512,128]{1,0:T(8,128)(2,1)S(1)}, u32[]{:S(2)}, u32[]{:S(2)}) collective-permute-start(bf16[512,128]{1,0:T(8,128)(2,1)} %x.3), channel_id=1, source_target_pairs={{0,32},{32,64},{64,96},{96,0},{1,33},{33,65},{65,97},{97,1},{2,34}... | collective-permute-start | bytes 393224 | tf_op jit(solution)/shard_map/ppermute | solution.py:217
  3.7 9.2 %collective-permute-start = (bf16[512,128]{1,0:T(8,128)(2,1)}, bf16[512,128]{1,0:T(8,128)(2,1)S(1)}, u32[]{:S(2)}, u32[]{:S(2)}) collective-permute-start(bf16[512,128]{1,0:T(8,128)(2,1)} %x.3), channel_id=1, source_target_pairs={{0,64},{32,96},{64,0},{96,32},{1,65},{33,97},{65,1},{97,33},{2,66}... | collective-permute-start | bytes 393224 | tf_op jit(solution)/shard_map/ppermute | solution.py:217
  16.5 2.7 %collective-permute-start.3 = (bf16[32,128,128]{2,1,0:T(8,128)(2,1)S(1)}, bf16[32,128,128]{2,1,0:T(8,128)(2,1)S(1)}, u32[]{:S(2)}, u32[]{:S(2)}) collective-permute-start(bf16[32,128,128]{2,1,0:T(8,128)(2,1)S(1)} %get-tuple-element.28), channel_id=1, source_target_pairs={{0,2},{2,0},{1,3},{3,1},{4,6},{6,4},{5,7},{7,5},{8,10},{10,8},{9,1... | collective-permute-start | bytes 3145736 | tf_op jit(solution)/shard_map/ppermute | solution.py:217
  19.3 28.5 %copy-start.1 = (bf16[512,128]{1,0:T(8,128)(2,1)S(1)}, bf16[512,128]{1,0:T(8,128)(2,1)}, u32[]{:S(2)}) copy-start(bf16[512,128]{1,0:T(8,128)(2,1)} %cot_a.1) | copy-start | bytes 393220
  19.3 28.5 %copy-start.2 = (bf16[128,128]{1,0:T(8,128)(2,1)S(1)}, bf16[128,128]{1,0:T(8,128)(2,1)}, u32[]{:S(2)}) copy-start(bf16[128,128]{1,0:T(8,128)(2,1)} %ws_a.3) | copy-start | bytes 98308
  19.3 28.5 %copy-start.3 = (bf16[128,128]{1,0:T(8,128)(2,1)S(1)}, bf16[128,128]{1,0:T(8,128)(2,1)}, u32[]{:S(2)}) copy-start(bf16[128,128]{1,0:T(8,128)(2,1)} %wn_a.1) | copy-start | bytes 98308
  19.3 28.5 %copy-start.5 = (f32[128]{0:T(128)S(1)}, f32[128]{0:T(128)}, u32[]{:S(2)}) copy-start(f32[128]{0:T(128)} %param.12) | copy-start | bytes 1540
  20.6 27.2 %all-to-all-start = ((bf16[16,256,128]{2,1,0:T(8,128)(2,1)}), bf16[16,256,128]{2,1,0:T(8,128)(2,1)S(1)}, u32[]{:S(2)}, u32[]{:S(2)}) async-start(bf16[16,256,128]{2,1,0:T(8,128)(2,1)} %bitcast.7), calls=%async_computation | async-start | bytes 2097152 | tf_op jit(solution)/shard_map/all_to_all | solution.py:321
  29.6 18.2 %collective-permute-start.4 = (bf16[528,128]{1,0:T(8,128)(2,1)S(1)}, bf16[528,128]{1,0:T(8,128)(2,1)S(1)}, u32[]{:S(2)}, u32[]{:S(2)}) collective-permute-start(bf16[528,128]{1,0:T(8,128)(2,1)S(1)} %get-tuple-element.29), channel_id=1, source_target_pairs={{0,1},{1,0},{2,3},{3,2},{4,5},{5,4},{6,7},{7,6},{8,9},{9,8},{10,11... | collective-permute-start | bytes 405512 | tf_op jit(solution)/shard_map/ppermute | solution.py:217
  50.0 5.7 %collective-permute-start.6 = (f32[2,136,128]{2,1,0:T(8,128)S(1)}, f32[2,136,128]{2,1,0:T(8,128)S(1)}, u32[]{:S(2)}, u32[]{:S(2)}) collective-permute-start(f32[2,136,128]{2,1,0:T(8,128)S(1)} %get-tuple-element.38), channel_id=1, source_target_pairs={{0,2},{2,0},{1,3},{3,1},{4,6},{6,4},{5,7},{7,5},{8,10},{10,8},{9,1... | collective-permute-start | bytes 417800 | tf_op jit(solution)/shard_map/ppermute | solution.py:217
  50.1 22.2 %all-to-all-start.1 = ((bf16[16,2,128,128]{3,2,1,0:T(8,128)(2,1)}), bf16[16,2,128,128]{3,2,1,0:T(8,128)(2,1)S(1)}, u32[]{:S(2)}, u32[]{:S(2)}) async-start(bf16[16,2,128,128]{3,2,1,0:T(8,128)(2,1)} %get-tuple-element.32), calls=%async_computation.1 | async-start | bytes 2097152 | tf_op jit(solution)/shard_map/all_to_all | solution.py:339
  55.7 4.8 %collective-permute-start.9 = (bf16[2,136,128]{2,1,0:T(8,128)(2,1)S(1)}, bf16[2,136,128]{2,1,0:T(8,128)(2,1)S(1)}, u32[]{:S(2)}, u32[]{:S(2)}) collective-permute-start(bf16[2,136,128]{2,1,0:T(8,128)(2,1)S(1)} %get-tuple-element.45), channel_id=1, source_target_pairs={{0,96},{32,0},{64,32},{96,64},{1,97},{33,1},{65,33},{97,65},{2,98}... | collective-permute-start | bytes 208904 | tf_op jit(solution)/shard_map/ppermute | solution.py:217
  56.9 6.5 %collective-permute-start.8 = (bf16[2,136,128]{2,1,0:T(8,128)(2,1)S(1)}, bf16[2,136,128]{2,1,0:T(8,128)(2,1)S(1)}, u32[]{:S(2)}, u32[]{:S(2)}) collective-permute-start(bf16[2,136,128]{2,1,0:T(8,128)(2,1)S(1)} %get-tuple-element.45), channel_id=1, source_target_pairs={{0,64},{32,96},{64,0},{96,32},{1,65},{33,97},{65,1},{97,33},{2,66}... | collective-permute-start | bytes 208904 | tf_op jit(solution)/shard_map/ppermute | solution.py:217
  56.9 6.8 %collective-permute-start.7 = (bf16[2,136,128]{2,1,0:T(8,128)(2,1)S(1)}, bf16[2,136,128]{2,1,0:T(8,128)(2,1)S(1)}, u32[]{:S(2)}, u32[]{:S(2)}) collective-permute-start(bf16[2,136,128]{2,1,0:T(8,128)(2,1)S(1)} %get-tuple-element.45), channel_id=1, source_target_pairs={{0,32},{32,64},{64,96},{96,0},{1,33},{33,65},{65,97},{97,1},{2,34}... | collective-permute-start | bytes 208904 | tf_op jit(solution)/shard_map/ppermute | solution.py:217
  63.7 7.1 %collective-permute-start.10 = (bf16[2,136,128]{2,1,0:T(8,128)(2,1)S(1)}, bf16[2,136,128]{2,1,0:T(8,128)(2,1)S(1)}, u32[]{:S(2)}, u32[]{:S(2)}) collective-permute-start(bf16[2,136,128]{2,1,0:T(8,128)(2,1)S(1)} %fusion), channel_id=1, source_target_pairs={{0,4},{4,0},{1,5},{5,1},{2,6},{6,2},{3,7},{7,3},{8,12},{12,8},{9,1... | collective-permute-start | bytes 208904 | tf_op jit(solution)/shard_map/ppermute | solution.py:217
  72.2 15.0 %collective-permute-start.11 = (bf16[32,128,128]{2,1,0:T(8,128)(2,1)S(1)}, bf16[32,128,128]{2,1,0:T(8,128)(2,1)S(1)}, u32[]{:S(2)}, u32[]{:S(2)}) collective-permute-start(bf16[32,128,128]{2,1,0:T(8,128)(2,1)S(1)} %bitcast.16), channel_id=1, source_target_pairs={{0,2},{2,0},{1,3},{3,1},{4,6},{6,4},{5,7},{7,5},{8,10},{10,8},{9,1... | collective-permute-start | bytes 3145736 | tf_op jit(solution)/shard_map/ppermute | solution.py:217
  72.2 6.0 %collective-permute-start.5 = (bf16[256,128]{1,0:T(8,128)(2,1)S(1)}, bf16[256,128]{1,0:T(8,128)(2,1)S(1)}, u32[]{:S(2)}, u32[]{:S(2)}) collective-permute-start(bf16[256,128]{1,0:T(8,128)(2,1)S(1)} %get-tuple-element.31), channel_id=1, source_target_pairs={{0,1},{1,0},{2,3},{3,2},{4,5},{5,4},{6,7},{7,6},{8,9},{9,8},{10,11... | collective-permute-start | bytes 196616 | tf_op jit(solution)/shard_map/ppermute | solution.py:217
  74.4 5.8 %collective-permute-start.12 = (f32[136,128]{1,0:T(8,128)S(1)}, f32[136,128]{1,0:T(8,128)S(1)}, u32[]{:S(2)}, u32[]{:S(2)}) collective-permute-start(f32[136,128]{1,0:T(8,128)S(1)} %slice_bitcast_fusion), channel_id=1, source_target_pairs={{0,1},{1,0},{2,3},{3,2},{4,5},{5,4},{6,7},{7,6},{8,9},{9,8},{10,11... | collective-permute-start | bytes 208904 | tf_op jit(solution)/shard_map/ppermute | solution.py:217
  80.2 17.6 %collective-permute-start.15 = (f32[136,128]{1,0:T(8,128)S(1)}, f32[136,128]{1,0:T(8,128)S(1)}, u32[]{:S(2)}, u32[]{:S(2)}) collective-permute-start(f32[136,128]{1,0:T(8,128)S(1)} %bitcast_add_fusion), channel_id=1, source_target_pairs={{0,24},{8,0},{16,8},{24,16},{1,25},{9,1},{17,9},{25,17},{2,26},{10... | collective-permute-start | bytes 208904 | tf_op jit(solution)/shard_map/ppermute | solution.py:217
  80.7 17.1 %collective-permute-start.14 = (f32[136,128]{1,0:T(8,128)S(1)}, f32[136,128]{1,0:T(8,128)S(1)}, u32[]{:S(2)}, u32[]{:S(2)}) collective-permute-start(f32[136,128]{1,0:T(8,128)S(1)} %bitcast_add_fusion), channel_id=1, source_target_pairs={{0,16},{8,24},{16,0},{24,8},{1,17},{9,25},{17,1},{25,9},{2,18},{10... | collective-permute-start | bytes 208904 | tf_op jit(solution)/shard_map/ppermute | solution.py:217
  83.7 14.1 %collective-permute-start.13 = (f32[136,128]{1,0:T(8,128)S(1)}, f32[136,128]{1,0:T(8,128)S(1)}, u32[]{:S(2)}, u32[]{:S(2)}) collective-permute-start(f32[136,128]{1,0:T(8,128)S(1)} %bitcast_add_fusion), channel_id=1, source_target_pairs={{0,8},{8,16},{16,24},{24,0},{1,9},{9,17},{17,25},{25,1},{2,10},{10... | collective-permute-start | bytes 208904 | tf_op jit(solution)/shard_map/ppermute | solution.py:217
  90.8 16.7 %all-to-all-start.2 = ((bf16[8,2,128,128]{3,2,1,0:T(8,128)(2,1)}), bf16[8,2,128,128]{3,2,1,0:T(8,128)(2,1)S(1)}, u32[]{:S(2)}, u32[]{:S(2)}) async-start(bf16[8,2,128,128]{3,2,1,0:T(8,128)(2,1)} %bitcast.9), calls=%async_computation.2 | async-start | bytes 1048576 | tf_op jit(solution)/shard_map/all_to_all | solution.py:385
  97.9 1.3 %collective-permute-start.16 = (f32[128,128]{1,0:T(8,128)S(1)}, f32[128,128]{1,0:T(8,128)S(1)}, u32[]{:S(2)}, u32[]{:S(2)}) collective-permute-start(f32[128,128]{1,0:T(8,128)S(1)} %slice.20), channel_id=1, source_target_pairs={{0,2},{2,0},{1,3},{3,1},{4,6},{6,4},{5,7},{7,5},{8,10},{10,8},{9,1... | collective-permute-start | bytes 196616 | tf_op jit(solution)/shard_map/ppermute | solution.py:217
  (3 other events, 34.0 us)
